TPU v7x, 256 devices: a whole 4x4x8 slice. The times are simulated.
256 devices in a mesh: member: 16 (over y, x_hi, core), domain: 16 (over x_lo, z).
Axes of the slice: x: 4 (x_hi: 2, x_lo: 2; x = x_hi * 2 + x_lo), y: 4, z: 8, core: 2. Of those that a mesh axis runs over, the one named last changes fastest.
Arguments:
- state: float32 [16, 4, 512, 512], P('member', None, 'domain'), may hold values from -5 to 5
- perturbation: float32 [16, 4, 512, 512], P('member', None, 'domain'), may hold values from -3 to 3
- parents: int32 [16], replicated, may hold values from 0 to 15
Outputs:
- final_state: float32 [16, 4, 512, 512], P('member', None, 'domain')
- score: float32 [16], P('member')
Inputs may be any that keep to these rules, and one draw needn't show every extreme that they name: `parents`: A member may be the parent of several slots or of none.
All inputs are finite; a program needn't handle non-finite values.
Results may differ from a plain program's by a relative error of at most 0.00002.
Values sent between devices are 32-bit elements; how exact they have to be, the bound alone decides.
A program may use at most 64 MiB of HBM per device.

v0:
```python
import jax
import jax.numpy as jnp
from jax import lax
from jax.sharding import PartitionSpec as P

STEPS = 3


time_step = 0.1
viscous = 0.05
coriolis = 1.0


def with_halo(cells, sides, width):
    for axis, dim in sides:
        count = lax.axis_size(axis)
        ends = count - 1
        head = lax.slice_in_dim(cells, 0, width, axis=dim)
        tail = lax.slice_in_dim(cells, cells.shape[dim] - width, cells.shape[dim], axis=dim)
        cells = jnp.concatenate(
            [
                lax.ppermute(tail, axis, [(i, (i + 1) % count) for i in range(ends)]),
                cells,
                lax.ppermute(head, axis, [((i + 1) % count, i) for i in range(ends)]),
            ],
            axis=dim,
        )
    return cells


def gradients(padded):
    middle = padded[:, 1:-1]
    east = jnp.roll(middle, -1, axis=-1)
    west = jnp.roll(middle, 1, axis=-1)
    return (middle, east, west, padded[:, 2:], padded[:, :-2])


def tendency(padded, start_row, total_rows):
    middle, east, west, north, south = gradients(padded)
    grad_x = (east - west) * 0.5
    grad_y = (north - south) * 0.5
    laplace = east + west + north + south - 4.0 * middle
    depth = 1.0 + padded[0]
    fluxes = jnp.stack([depth * padded[1], depth * padded[2]])
    flux_mid, flux_east, flux_west, flux_north, flux_south = gradients(fluxes)
    count = padded.shape[1] - 2
    global_rows = (start_row + 1 + jnp.arange(count, dtype=jnp.int32)).astype(jnp.float32)
    latitude = coriolis * (2.0 * (global_rows + 0.5) / total_rows - 1.0)
    latitude = latitude[:, None]
    height, speed_u, speed_v, tracer = (middle[0], middle[1], middle[2], middle[3])
    advect = speed_u * grad_x + speed_v * grad_y
    d_eta = (
        -((flux_east[0] - flux_west[0]) * 0.5 + (flux_north[1] - flux_south[1]) * 0.5)
        + viscous * laplace[0]
    )
    d_u = -advect[1] + latitude * speed_v - grad_x[0] + viscous * laplace[1]
    d_v = -advect[2] - latitude * speed_u - grad_y[0] + viscous * laplace[2]
    d_q = -advect[3] + viscous * laplace[3]
    return jnp.stack([d_eta, d_u, d_v, d_q])


def section_operator(field, first_row, total_rows):
    padded = with_halo(field, (("domain", 1),), 1)
    return tendency(padded, first_row - 1, total_rows)


def step_shallow(field, first_row, total_rows):
    start = section_operator(field, first_row, total_rows)
    first = field + time_step * start
    second = 0.75 * field + 0.25 * (
        first + time_step * section_operator(first, first_row, total_rows)
    )
    return 1.0 / 3.0 * field + 2.0 / 3.0 * (
        second + time_step * section_operator(second, first_row, total_rows)
    )


def run_steps(field, first_row, total_rows):
    for count in range(STEPS):
        field = step_shallow(field, first_row, total_rows)
    return field


def on_device(state, perturbation, parents):
    rows = state.shape[2]
    width = state.shape[3]
    total_rows = rows * lax.axis_size("domain")
    first_row = lax.axis_index("domain") * rows
    before = run_steps(state[0], first_row, total_rows)
    global_rows = (first_row + jnp.arange(rows, dtype=jnp.int32)).astype(jnp.float32)
    weight = 1.0 + 2.0 * global_rows / (total_rows - 1)
    local_score = jnp.sum(weight[:, None] * before[3] * before[3])
    score = lax.psum(local_score, "domain") / (total_rows * width)
    parent = lax.dynamic_index_in_dim(parents, lax.axis_index("member"), 0, keepdims=False)
    piece = lax.all_gather(before[None], "member", axis=0, tiled=True)
    count = piece.shape[0]
    inside = (parent >= 0) & (parent < count)
    chosen = lax.dynamic_index_in_dim(piece, jnp.clip(parent, 0, count - 1), 0, keepdims=False)
    cloned = jnp.where(inside, chosen, jnp.zeros_like(before))
    after = run_steps(cloned + perturbation[0], first_row, total_rows)
    return (after[None], jnp.reshape(score, (1,)))


def solution(mesh):
    placed = (P("member", None, "domain", None), P("member", None, "domain", None), P())
    return jax.shard_map(
        on_device,
        mesh=mesh,
        in_specs=placed,
        out_specs=(P("member", None, "domain", None), P("member")),
        check_vma=False,
    )
```

profile of v0, /device:TPU:2, one launch (start us, length us, event | category | flops | bytes accessed | tf_op | source)
XLA Modules:
  0.0 271.7 jit_solution(4103556976015861069)
XLA Ops:
  8.1 3.8 %collective-permute-start = (f32[4,1,512]{2,1,0:T(1,128)S(1)}, f32[4,1,512]{2,1,0:T(1,128)S(1)}, u32[]{:S(2)}, u32[]{:S(2)}) collective-permute-start(f32[4,1,512]{2,1,0:T(1,128)S(1)} %get-tuple-element.324), channel_id=1, source_target_pairs={{0,1},{1,2},{2,3},{3,4},{4,5},{5,6},{6,7},{7,8},{8,9},{9,10},{10,1... | collective-permute-start | bytes 24584 | tf_op jit(solution)/shard_map/ppermute | solution.py:22
  12.0 5.8 %collective-permute-start.1 = (f32[4,1,512]{2,1,0:T(1,128)S(1)}, f32[4,1,512]{2,1,0:T(1,128)S(1)}, u32[]{:S(2)}, u32[]{:S(2)}) collective-permute-start(f32[4,1,512]{2,1,0:T(1,128)S(1)} %get-tuple-element.325), channel_id=1, source_target_pairs={{1,0},{2,1},{3,2},{4,3},{5,4},{6,5},{7,6},{8,7},{9,8},{10,9},{11,1... | collective-permute-start | bytes 24584 | tf_op jit(solution)/shard_map/ppermute | solution.py:24
  22.0 1.4 multiply_add_fusion.17
  23.8 1.9 collective-permute-start.2
  25.7 6.0 %collective-permute-start.3 = (f32[4,1,512]{2,1,0:T(1,128)S(1)}, f32[4,1,512]{2,1,0:T(1,128)S(1)}, u32[]{:S(2)}, u32[]{:S(2)}) collective-permute-start(f32[4,1,512]{2,1,0:T(1,128)S(1)} %get-tuple-element.316), channel_id=1, source_target_pairs={{1,0},{2,1},{3,2},{4,3},{5,4},{6,5},{7,6},{8,7},{9,8},{10,9},{11,1... | collective-permute-start | bytes 24584 | tf_op jit(solution)/shard_map/ppermute | solution.py:24
  31.8 1.3 collective-permute-done.3
  34.0 2.9 %collective-permute-start.4 = (f32[4,1,512]{2,1,0:T(1,128)S(1)}, f32[4,1,512]{2,1,0:T(1,128)S(1)}, u32[]{:S(2)}, u32[]{:S(2)}) collective-permute-start(f32[4,1,512]{2,1,0:T(1,128)S(1)} %get-tuple-element.306), channel_id=1, source_target_pairs={{0,1},{1,2},{2,3},{3,4},{4,5},{5,6},{6,7},{7,8},{8,9},{9,10},{10,1... | collective-permute-start | bytes 24584 | tf_op jit(solution)/shard_map/ppermute | solution.py:22
  36.8 5.4 %collective-permute-start.5 = (f32[4,1,512]{2,1,0:T(1,128)S(1)}, f32[4,1,512]{2,1,0:T(1,128)S(1)}, u32[]{:S(2)}, u32[]{:S(2)}) collective-permute-start(f32[4,1,512]{2,1,0:T(1,128)S(1)} %get-tuple-element.307), channel_id=1, source_target_pairs={{1,0},{2,1},{3,2},{4,3},{5,4},{6,5},{7,6},{8,7},{9,8},{10,9},{11,1... | collective-permute-start | bytes 24584 | tf_op jit(solution)/shard_map/ppermute | solution.py:24
  42.3 1.3 collective-permute-done.5
  44.5 3.4 %collective-permute-start.6 = (f32[4,1,512]{2,1,0:T(1,128)S(1)}, f32[4,1,512]{2,1,0:T(1,128)S(1)}, u32[]{:S(2)}, u32[]{:S(2)}) collective-permute-start(f32[4,1,512]{2,1,0:T(1,128)S(1)} %get-tuple-element.297), channel_id=1, source_target_pairs={{0,1},{1,2},{2,3},{3,4},{4,5},{5,6},{6,7},{7,8},{8,9},{9,10},{10,1... | collective-permute-start | bytes 24584 | tf_op jit(solution)/shard_map/ppermute | solution.py:22
  47.9 4.8 %collective-permute-start.7 = (f32[4,1,512]{2,1,0:T(1,128)S(1)}, f32[4,1,512]{2,1,0:T(1,128)S(1)}, u32[]{:S(2)}, u32[]{:S(2)}) collective-permute-start(f32[4,1,512]{2,1,0:T(1,128)S(1)} %get-tuple-element.298), channel_id=1, source_target_pairs={{1,0},{2,1},{3,2},{4,3},{5,4},{6,5},{7,6},{8,7},{9,8},{10,9},{11,1... | collective-permute-start | bytes 24584 | tf_op jit(solution)/shard_map/ppermute | solution.py:24
  52.8 1.3 collective-permute-done.7
  54.9 3.3 %collective-permute-start.8 = (f32[4,1,512]{2,1,0:T(1,128)S(1)}, f32[4,1,512]{2,1,0:T(1,128)S(1)}, u32[]{:S(2)}, u32[]{:S(2)}) collective-permute-start(f32[4,1,512]{2,1,0:T(1,128)S(1)} %get-tuple-element.288), channel_id=1, source_target_pairs={{0,1},{1,2},{2,3},{3,4},{4,5},{5,6},{6,7},{7,8},{8,9},{9,10},{10,1... | collective-permute-start | bytes 24584 | tf_op jit(solution)/shard_map/ppermute | solution.py:22
  58.2 4.9 %collective-permute-start.9 = (f32[4,1,512]{2,1,0:T(1,128)S(1)}, f32[4,1,512]{2,1,0:T(1,128)S(1)}, u32[]{:S(2)}, u32[]{:S(2)}) collective-permute-start(f32[4,1,512]{2,1,0:T(1,128)S(1)} %get-tuple-element.289), channel_id=1, source_target_pairs={{1,0},{2,1},{3,2},{4,3},{5,4},{6,5},{7,6},{8,7},{9,8},{10,9},{11,1... | collective-permute-start | bytes 24584 | tf_op jit(solution)/shard_map/ppermute | solution.py:24
  63.2 1.3 collective-permute-done.9
  65.4 2.4 collective-permute-start.10
  67.8 5.8 %collective-permute-start.11 = (f32[4,1,512]{2,1,0:T(1,128)S(1)}, f32[4,1,512]{2,1,0:T(1,128)S(1)}, u32[]{:S(2)}, u32[]{:S(2)}) collective-permute-start(f32[4,1,512]{2,1,0:T(1,128)S(1)} %get-tuple-element.280), channel_id=1, source_target_pairs={{1,0},{2,1},{3,2},{4,3},{5,4},{6,5},{7,6},{8,7},{9,8},{10,9},{11,1... | collective-permute-start | bytes 24584 | tf_op jit(solution)/shard_map/ppermute | solution.py:24
  73.7 1.3 collective-permute-done.11
  75.9 1.9 collective-permute-start.12
  77.8 6.3 %collective-permute-start.13 = (f32[4,1,512]{2,1,0:T(1,128)S(1)}, f32[4,1,512]{2,1,0:T(1,128)S(1)}, u32[]{:S(2)}, u32[]{:S(2)}) collective-permute-start(f32[4,1,512]{2,1,0:T(1,128)S(1)} %get-tuple-element.271), channel_id=1, source_target_pairs={{1,0},{2,1},{3,2},{4,3},{5,4},{6,5},{7,6},{8,7},{9,8},{10,9},{11,1... | collective-permute-start | bytes 24584 | tf_op jit(solution)/shard_map/ppermute | solution.py:24
  84.2 1.3 collective-permute-done.13
  86.3 1.9 collective-permute-start.14
  88.2 6.3 %collective-permute-start.15 = (f32[4,1,512]{2,1,0:T(1,128)S(1)}, f32[4,1,512]{2,1,0:T(1,128)S(1)}, u32[]{:S(2)}, u32[]{:S(2)}) collective-permute-start(f32[4,1,512]{2,1,0:T(1,128)S(1)} %get-tuple-element.262), channel_id=1, source_target_pairs={{1,0},{2,1},{3,2},{4,3},{5,4},{6,5},{7,6},{8,7},{9,8},{10,9},{11,1... | collective-permute-start | bytes 24584 | tf_op jit(solution)/shard_map/ppermute | solution.py:24
  94.6 1.3 collective-permute-done.15
  96.8 1.9 collective-permute-start.16
  98.7 6.4 %collective-permute-start.17 = (f32[4,1,512]{2,1,0:T(1,128)S(1)}, f32[4,1,512]{2,1,0:T(1,128)S(1)}, u32[]{:S(2)}, u32[]{:S(2)}) collective-permute-start(f32[4,1,512]{2,1,0:T(1,128)S(1)} %get-tuple-element.253), channel_id=1, source_target_pairs={{1,0},{2,1},{3,2},{4,3},{5,4},{6,5},{7,6},{8,7},{9,8},{10,9},{11,1... | collective-permute-start | bytes 24584 | tf_op jit(solution)/shard_map/ppermute | solution.py:24
  111.5 35.7 %psum.7 = f32[]{:T(128)} all-reduce(f32[]{:T(128)} %fusion.150), channel_id=1, replica_groups=mesh['member'=16,'domain'=16] {'domain'}, use_global_device_ids=true, to_apply=%region_1.2 | all-reduce | flops 1 | bytes 8 | tf_op jit(solution)/shard_map/psum | solution.py:93
  147.9 19.7 %all-gather.2.cloned.1.call-done = f32[16,4,32,512]{3,2,1,0:T(8,128)} async-done(((f32[1,4,32,512]{3,2,1,0:T(8,128)}), f32[16,4,32,512]{3,2,1,0:T(8,128)}) %all-gather.2.cloned.1.call-update) | async-done | bytes 4194320 | tf_op jit(solution)/shard_map/all_gather | solution.py:95
  168.7 3.5 %collective-permute-start.18 = (f32[4,1,512]{2,1,0:T(1,128)S(1)}, f32[4,1,512]{2,1,0:T(1,128)S(1)}, u32[]{:S(2)}, u32[]{:S(2)}) collective-permute-start(f32[4,1,512]{2,1,0:T(1,128)S(1)} %get-tuple-element.243), channel_id=1, source_target_pairs={{0,1},{1,2},{2,3},{3,4},{4,5},{5,6},{6,7},{7,8},{8,9},{9,10},{10,1... | collective-permute-start | bytes 24584 | tf_op jit(solution)/shard_map/ppermute | solution.py:22
  172.2 4.6 %collective-permute-start.19 = (f32[4,1,512]{2,1,0:T(1,128)S(1)}, f32[4,1,512]{2,1,0:T(1,128)S(1)}, u32[]{:S(2)}, u32[]{:S(2)}) collective-permute-start(f32[4,1,512]{2,1,0:T(1,128)S(1)} %get-tuple-element.244), channel_id=1, source_target_pairs={{1,0},{2,1},{3,2},{4,3},{5,4},{6,5},{7,6},{8,7},{9,8},{10,9},{11,1... | collective-permute-start | bytes 24584 | tf_op jit(solution)/shard_map/ppermute | solution.py:24
  179.0 3.1 %collective-permute-start.20 = (f32[4,1,512]{2,1,0:T(1,128)S(1)}, f32[4,1,512]{2,1,0:T(1,128)S(1)}, u32[]{:S(2)}, u32[]{:S(2)}) collective-permute-start(f32[4,1,512]{2,1,0:T(1,128)S(1)} %get-tuple-element.234), channel_id=1, source_target_pairs={{0,1},{1,2},{2,3},{3,4},{4,5},{5,6},{6,7},{7,8},{8,9},{9,10},{10,1... | collective-permute-start | bytes 24584 | tf_op jit(solution)/shard_map/ppermute | solution.py:22
  182.0 5.1 %collective-permute-start.21 = (f32[4,1,512]{2,1,0:T(1,128)S(1)}, f32[4,1,512]{2,1,0:T(1,128)S(1)}, u32[]{:S(2)}, u32[]{:S(2)}) collective-permute-start(f32[4,1,512]{2,1,0:T(1,128)S(1)} %get-tuple-element.235), channel_id=1, source_target_pairs={{1,0},{2,1},{3,2},{4,3},{5,4},{6,5},{7,6},{8,7},{9,8},{10,9},{11,1... | collective-permute-start | bytes 24584 | tf_op jit(solution)/shard_map/ppermute | solution.py:24
  189.4 4.5 %collective-permute-start.22 = (f32[4,1,512]{2,1,0:T(1,128)S(1)}, f32[4,1,512]{2,1,0:T(1,128)S(1)}, u32[]{:S(2)}, u32[]{:S(2)}) collective-permute-start(f32[4,1,512]{2,1,0:T(1,128)S(1)} %get-tuple-element.225), channel_id=1, source_target_pairs={{0,1},{1,2},{2,3},{3,4},{4,5},{5,6},{6,7},{7,8},{8,9},{9,10},{10,1... | collective-permute-start | bytes 24584 | tf_op jit(solution)/shard_map/ppermute | solution.py:22
  193.9 3.7 %collective-permute-start.23 = (f32[4,1,512]{2,1,0:T(1,128)S(1)}, f32[4,1,512]{2,1,0:T(1,128)S(1)}, u32[]{:S(2)}, u32[]{:S(2)}) collective-permute-start(f32[4,1,512]{2,1,0:T(1,128)S(1)} %get-tuple-element.226), channel_id=1, source_target_pairs={{1,0},{2,1},{3,2},{4,3},{5,4},{6,5},{7,6},{8,7},{9,8},{10,9},{11,1... | collective-permute-start | bytes 24584 | tf_op jit(solution)/shard_map/ppermute | solution.py:24
  197.7 1.7 collective-permute-done.23
  200.4 3.9 %collective-permute-start.24 = (f32[4,1,512]{2,1,0:T(1,128)S(1)}, f32[4,1,512]{2,1,0:T(1,128)S(1)}, u32[]{:S(2)}, u32[]{:S(2)}) collective-permute-start(f32[4,1,512]{2,1,0:T(1,128)S(1)} %get-tuple-element.216), channel_id=1, source_target_pairs={{0,1},{1,2},{2,3},{3,4},{4,5},{5,6},{6,7},{7,8},{8,9},{9,10},{10,1... | collective-permute-start | bytes 24584 | tf_op jit(solution)/shard_map/ppermute | solution.py:22
  204.3 4.0 %collective-permute-start.25 = (f32[4,1,512]{2,1,0:T(1,128)S(1)}, f32[4,1,512]{2,1,0:T(1,128)S(1)}, u32[]{:S(2)}, u32[]{:S(2)}) collective-permute-start(f32[4,1,512]{2,1,0:T(1,128)S(1)} %get-tuple-element.217), channel_id=1, source_target_pairs={{1,0},{2,1},{3,2},{4,3},{5,4},{6,5},{7,6},{8,7},{9,8},{10,9},{11,1... | collective-permute-start | bytes 24584 | tf_op jit(solution)/shard_map/ppermute | solution.py:24
  208.4 1.4 collective-permute-done.25
  210.7 3.1 %collective-permute-start.26 = (f32[4,1,512]{2,1,0:T(1,128)S(1)}, f32[4,1,512]{2,1,0:T(1,128)S(1)}, u32[]{:S(2)}, u32[]{:S(2)}) collective-permute-start(f32[4,1,512]{2,1,0:T(1,128)S(1)} %get-tuple-element.207), channel_id=1, source_target_pairs={{0,1},{1,2},{2,3},{3,4},{4,5},{5,6},{6,7},{7,8},{8,9},{9,10},{10,1... | collective-permute-start | bytes 24584 | tf_op jit(solution)/shard_map/ppermute | solution.py:22
  213.8 5.1 %collective-permute-start.27 = (f32[4,1,512]{2,1,0:T(1,128)S(1)}, f32[4,1,512]{2,1,0:T(1,128)S(1)}, u32[]{:S(2)}, u32[]{:S(2)}) collective-permute-start(f32[4,1,512]{2,1,0:T(1,128)S(1)} %get-tuple-element.208), channel_id=1, source_target_pairs={{1,0},{2,1},{3,2},{4,3},{5,4},{6,5},{7,6},{8,7},{9,8},{10,9},{11,1... | collective-permute-start | bytes 24584 | tf_op jit(solution)/shard_map/ppermute | solution.py:24
  221.0 2.4 collective-permute-start.28
  223.4 5.8 %collective-permute-start.29 = (f32[4,1,512]{2,1,0:T(1,128)S(1)}, f32[4,1,512]{2,1,0:T(1,128)S(1)}, u32[]{:S(2)}, u32[]{:S(2)}) collective-permute-start(f32[4,1,512]{2,1,0:T(1,128)S(1)} %get-tuple-element.199), channel_id=1, source_target_pairs={{1,0},{2,1},{3,2},{4,3},{5,4},{6,5},{7,6},{8,7},{9,8},{10,9},{11,1... | collective-permute-start | bytes 24584 | tf_op jit(solution)/shard_map/ppermute | solution.py:24
  231.5 1.9 collective-permute-start.30
  233.4 6.3 %collective-permute-start.31 = (f32[4,1,512]{2,1,0:T(1,128)S(1)}, f32[4,1,512]{2,1,0:T(1,128)S(1)}, u32[]{:S(2)}, u32[]{:S(2)}) collective-permute-start(f32[4,1,512]{2,1,0:T(1,128)S(1)} %get-tuple-element.190), channel_id=1, source_target_pairs={{1,0},{2,1},{3,2},{4,3},{5,4},{6,5},{7,6},{8,7},{9,8},{10,9},{11,1... | collective-permute-start | bytes 24584 | tf_op jit(solution)/shard_map/ppermute | solution.py:24
  241.9 1.9 collective-permute-start.32
  243.8 6.3 %collective-permute-start.33 = (f32[4,1,512]{2,1,0:T(1,128)S(1)}, f32[4,1,512]{2,1,0:T(1,128)S(1)}, u32[]{:S(2)}, u32[]{:S(2)}) collective-permute-start(f32[4,1,512]{2,1,0:T(1,128)S(1)} %get-tuple-element.181), channel_id=1, source_target_pairs={{1,0},{2,1},{3,2},{4,3},{5,4},{6,5},{7,6},{8,7},{9,8},{10,9},{11,1... | collective-permute-start | bytes 24584 | tf_op jit(solution)/shard_map/ppermute | solution.py:24
  252.4 1.9 collective-permute-start.34
  254.3 6.3 %collective-permute-start.35 = (f32[4,1,512]{2,1,0:T(1,128)S(1)}, f32[4,1,512]{2,1,0:T(1,128)S(1)}, u32[]{:S(2)}, u32[]{:S(2)}) collective-permute-start(f32[4,1,512]{2,1,0:T(1,128)S(1)} %get-tuple-element.172), channel_id=1, source_target_pairs={{1,0},{2,1},{3,2},{4,3},{5,4},{6,5},{7,6},{8,7},{9,8},{10,9},{11,1... | collective-permute-start | bytes 24584 | tf_op jit(solution)/shard_map/ppermute | solution.py:24
  (219 shorter events, 35.0 us)
Async XLA Ops:
  7.2 16.2 %copy-start = (f32[1,4,32,512]{3,2,1,0:T(8,128)S(1)}, f32[1,4,32,512]{3,2,1,0:T(8,128)}, u32[]{:S(2)}) copy-start(f32[1,4,32,512]{3,2,1,0:T(8,128)} %param.3) | copy-start | bytes 786436
  7.2 160.4 %all-gather.2.cloned.1.call-start = ((), (), s32[]{:S(2)}) async-start(), calls=%async_computation | async-start | bytes 4456448 | tf_op jit(solution)/shard_map/all_gather | solution.py:95
  8.1 12.7 %collective-permute-start = (f32[4,1,512]{2,1,0:T(1,128)S(1)}, f32[4,1,512]{2,1,0:T(1,128)S(1)}, u32[]{:S(2)}, u32[]{:S(2)}) collective-permute-start(f32[4,1,512]{2,1,0:T(1,128)S(1)} %get-tuple-element.324), channel_id=1, source_target_pairs={{0,1},{1,2},{2,3},{3,4},{4,5},{5,6},{6,7},{7,8},{8,9},{9,10},{10,1... | collective-permute-start | bytes 24584 | tf_op jit(solution)/shard_map/ppermute | solution.py:22
  12.0 8.9 %collective-permute-start.1 = (f32[4,1,512]{2,1,0:T(1,128)S(1)}, f32[4,1,512]{2,1,0:T(1,128)S(1)}, u32[]{:S(2)}, u32[]{:S(2)}) collective-permute-start(f32[4,1,512]{2,1,0:T(1,128)S(1)} %get-tuple-element.325), channel_id=1, source_target_pairs={{1,0},{2,1},{3,2},{4,3},{5,4},{6,5},{7,6},{8,7},{9,8},{10,9},{11,1... | collective-permute-start | bytes 24584 | tf_op jit(solution)/shard_map/ppermute | solution.py:24
  23.8 8.1 %collective-permute-start.2 = (f32[4,1,512]{2,1,0:T(1,128)S(1)}, f32[4,1,512]{2,1,0:T(1,128)S(1)}, u32[]{:S(2)}, u32[]{:S(2)}) collective-permute-start(f32[4,1,512]{2,1,0:T(1,128)S(1)} %get-tuple-element.315), channel_id=1, source_target_pairs={{0,1},{1,2},{2,3},{3,4},{4,5},{5,6},{6,7},{7,8},{8,9},{9,10},{10,1... | collective-permute-start | bytes 24584 | tf_op jit(solution)/shard_map/ppermute | solution.py:22
  25.7 7.4 %collective-permute-start.3 = (f32[4,1,512]{2,1,0:T(1,128)S(1)}, f32[4,1,512]{2,1,0:T(1,128)S(1)}, u32[]{:S(2)}, u32[]{:S(2)}) collective-permute-start(f32[4,1,512]{2,1,0:T(1,128)S(1)} %get-tuple-element.316), channel_id=1, source_target_pairs={{1,0},{2,1},{3,2},{4,3},{5,4},{6,5},{7,6},{8,7},{9,8},{10,9},{11,1... | collective-permute-start | bytes 24584 | tf_op jit(solution)/shard_map/ppermute | solution.py:24
  34.0 8.3 %collective-permute-start.4 = (f32[4,1,512]{2,1,0:T(1,128)S(1)}, f32[4,1,512]{2,1,0:T(1,128)S(1)}, u32[]{:S(2)}, u32[]{:S(2)}) collective-permute-start(f32[4,1,512]{2,1,0:T(1,128)S(1)} %get-tuple-element.306), channel_id=1, source_target_pairs={{0,1},{1,2},{2,3},{3,4},{4,5},{5,6},{6,7},{7,8},{8,9},{9,10},{10,1... | collective-permute-start | bytes 24584 | tf_op jit(solution)/shard_map/ppermute | solution.py:22
  36.8 6.7 %collective-permute-start.5 = (f32[4,1,512]{2,1,0:T(1,128)S(1)}, f32[4,1,512]{2,1,0:T(1,128)S(1)}, u32[]{:S(2)}, u32[]{:S(2)}) collective-permute-start(f32[4,1,512]{2,1,0:T(1,128)S(1)} %get-tuple-element.307), channel_id=1, source_target_pairs={{1,0},{2,1},{3,2},{4,3},{5,4},{6,5},{7,6},{8,7},{9,8},{10,9},{11,1... | collective-permute-start | bytes 24584 | tf_op jit(solution)/shard_map/ppermute | solution.py:24
  44.5 8.3 %collective-permute-start.6 = (f32[4,1,512]{2,1,0:T(1,128)S(1)}, f32[4,1,512]{2,1,0:T(1,128)S(1)}, u32[]{:S(2)}, u32[]{:S(2)}) collective-permute-start(f32[4,1,512]{2,1,0:T(1,128)S(1)} %get-tuple-element.297), channel_id=1, source_target_pairs={{0,1},{1,2},{2,3},{3,4},{4,5},{5,6},{6,7},{7,8},{8,9},{9,10},{10,1... | collective-permute-start | bytes 24584 | tf_op jit(solution)/shard_map/ppermute | solution.py:22
  47.9 6.2 %collective-permute-start.7 = (f32[4,1,512]{2,1,0:T(1,128)S(1)}, f32[4,1,512]{2,1,0:T(1,128)S(1)}, u32[]{:S(2)}, u32[]{:S(2)}) collective-permute-start(f32[4,1,512]{2,1,0:T(1,128)S(1)} %get-tuple-element.298), channel_id=1, source_target_pairs={{1,0},{2,1},{3,2},{4,3},{5,4},{6,5},{7,6},{8,7},{9,8},{10,9},{11,1... | collective-permute-start | bytes 24584 | tf_op jit(solution)/shard_map/ppermute | solution.py:24
  54.9 8.3 %collective-permute-start.8 = (f32[4,1,512]{2,1,0:T(1,128)S(1)}, f32[4,1,512]{2,1,0:T(1,128)S(1)}, u32[]{:S(2)}, u32[]{:S(2)}) collective-permute-start(f32[4,1,512]{2,1,0:T(1,128)S(1)} %get-tuple-element.288), channel_id=1, source_target_pairs={{0,1},{1,2},{2,3},{3,4},{4,5},{5,6},{6,7},{7,8},{8,9},{9,10},{10,1... | collective-permute-start | bytes 24584 | tf_op jit(solution)/shard_map/ppermute | solution.py:22
  58.2 6.3 %collective-permute-start.9 = (f32[4,1,512]{2,1,0:T(1,128)S(1)}, f32[4,1,512]{2,1,0:T(1,128)S(1)}, u32[]{:S(2)}, u32[]{:S(2)}) collective-permute-start(f32[4,1,512]{2,1,0:T(1,128)S(1)} %get-tuple-element.289), channel_id=1, source_target_pairs={{1,0},{2,1},{3,2},{4,3},{5,4},{6,5},{7,6},{8,7},{9,8},{10,9},{11,1... | collective-permute-start | bytes 24584 | tf_op jit(solution)/shard_map/ppermute | solution.py:24
  65.4 8.3 %collective-permute-start.10 = (f32[4,1,512]{2,1,0:T(1,128)S(1)}, f32[4,1,512]{2,1,0:T(1,128)S(1)}, u32[]{:S(2)}, u32[]{:S(2)}) collective-permute-start(f32[4,1,512]{2,1,0:T(1,128)S(1)} %get-tuple-element.279), channel_id=1, source_target_pairs={{0,1},{1,2},{2,3},{3,4},{4,5},{5,6},{6,7},{7,8},{8,9},{9,10},{10,1... | collective-permute-start | bytes 24584 | tf_op jit(solution)/shard_map/ppermute | solution.py:22
  67.8 7.2 %collective-permute-start.11 = (f32[4,1,512]{2,1,0:T(1,128)S(1)}, f32[4,1,512]{2,1,0:T(1,128)S(1)}, u32[]{:S(2)}, u32[]{:S(2)}) collective-permute-start(f32[4,1,512]{2,1,0:T(1,128)S(1)} %get-tuple-element.280), channel_id=1, source_target_pairs={{1,0},{2,1},{3,2},{4,3},{5,4},{6,5},{7,6},{8,7},{9,8},{10,9},{11,1... | collective-permute-start | bytes 24584 | tf_op jit(solution)/shard_map/ppermute | solution.py:24
  75.9 8.3 %collective-permute-start.12 = (f32[4,1,512]{2,1,0:T(1,128)S(1)}, f32[4,1,512]{2,1,0:T(1,128)S(1)}, u32[]{:S(2)}, u32[]{:S(2)}) collective-permute-start(f32[4,1,512]{2,1,0:T(1,128)S(1)} %get-tuple-element.270), channel_id=1, source_target_pairs={{0,1},{1,2},{2,3},{3,4},{4,5},{5,6},{6,7},{7,8},{8,9},{9,10},{10,1... | collective-permute-start | bytes 24584 | tf_op jit(solution)/shard_map/ppermute | solution.py:22
  77.8 7.7 %collective-permute-start.13 = (f32[4,1,512]{2,1,0:T(1,128)S(1)}, f32[4,1,512]{2,1,0:T(1,128)S(1)}, u32[]{:S(2)}, u32[]{:S(2)}) collective-permute-start(f32[4,1,512]{2,1,0:T(1,128)S(1)} %get-tuple-element.271), channel_id=1, source_target_pairs={{1,0},{2,1},{3,2},{4,3},{5,4},{6,5},{7,6},{8,7},{9,8},{10,9},{11,1... | collective-permute-start | bytes 24584 | tf_op jit(solution)/shard_map/ppermute | solution.py:24
  86.3 8.3 %collective-permute-start.14 = (f32[4,1,512]{2,1,0:T(1,128)S(1)}, f32[4,1,512]{2,1,0:T(1,128)S(1)}, u32[]{:S(2)}, u32[]{:S(2)}) collective-permute-start(f32[4,1,512]{2,1,0:T(1,128)S(1)} %get-tuple-element.261), channel_id=1, source_target_pairs={{0,1},{1,2},{2,3},{3,4},{4,5},{5,6},{6,7},{7,8},{8,9},{9,10},{10,1... | collective-permute-start | bytes 24584 | tf_op jit(solution)/shard_map/ppermute | solution.py:22
  88.2 7.7 %collective-permute-start.15 = (f32[4,1,512]{2,1,0:T(1,128)S(1)}, f32[4,1,512]{2,1,0:T(1,128)S(1)}, u32[]{:S(2)}, u32[]{:S(2)}) collective-permute-start(f32[4,1,512]{2,1,0:T(1,128)S(1)} %get-tuple-element.262), channel_id=1, source_target_pairs={{1,0},{2,1},{3,2},{4,3},{5,4},{6,5},{7,6},{8,7},{9,8},{10,9},{11,1... | collective-permute-start | bytes 24584 | tf_op jit(solution)/shard_map/ppermute | solution.py:24
  96.7 11.5 %copy-start.2 = (s32[16]{0:T(128)S(1)}, s32[16]{0:T(128)}, u32[]{:S(2)}) copy-start(s32[16]{0:T(128)} %param.5) | copy-start | bytes 196
  96.8 8.5 %collective-permute-start.16 = (f32[4,1,512]{2,1,0:T(1,128)S(1)}, f32[4,1,512]{2,1,0:T(1,128)S(1)}, u32[]{:S(2)}, u32[]{:S(2)}) collective-permute-start(f32[4,1,512]{2,1,0:T(1,128)S(1)} %get-tuple-element.252), channel_id=1, source_target_pairs={{0,1},{1,2},{2,3},{3,4},{4,5},{5,6},{6,7},{7,8},{8,9},{9,10},{10,1... | collective-permute-start | bytes 24584 | tf_op jit(solution)/shard_map/ppermute | solution.py:22
  98.7 68.8 %copy-start.1 = (f32[1,4,32,512]{3,2,1,0:T(8,128)S(1)}, f32[1,4,32,512]{3,2,1,0:T(8,128)}, u32[]{:S(2)}) copy-start(f32[1,4,32,512]{3,2,1,0:T(8,128)} %param.4) | copy-start | bytes 786436
  98.7 7.8 %collective-permute-start.17 = (f32[4,1,512]{2,1,0:T(1,128)S(1)}, f32[4,1,512]{2,1,0:T(1,128)S(1)}, u32[]{:S(2)}, u32[]{:S(2)}) collective-permute-start(f32[4,1,512]{2,1,0:T(1,128)S(1)} %get-tuple-element.253), channel_id=1, source_target_pairs={{1,0},{2,1},{3,2},{4,3},{5,4},{6,5},{7,6},{8,7},{9,8},{10,9},{11,1... | collective-permute-start | bytes 24584 | tf_op jit(solution)/shard_map/ppermute | solution.py:24
  168.7 8.1 %collective-permute-start.18 = (f32[4,1,512]{2,1,0:T(1,128)S(1)}, f32[4,1,512]{2,1,0:T(1,128)S(1)}, u32[]{:S(2)}, u32[]{:S(2)}) collective-permute-start(f32[4,1,512]{2,1,0:T(1,128)S(1)} %get-tuple-element.243), channel_id=1, source_target_pairs={{0,1},{1,2},{2,3},{3,4},{4,5},{5,6},{6,7},{7,8},{8,9},{9,10},{10,1... | collective-permute-start | bytes 24584 | tf_op jit(solution)/shard_map/ppermute | solution.py:22
  172.2 5.9 %collective-permute-start.19 = (f32[4,1,512]{2,1,0:T(1,128)S(1)}, f32[4,1,512]{2,1,0:T(1,128)S(1)}, u32[]{:S(2)}, u32[]{:S(2)}) collective-permute-start(f32[4,1,512]{2,1,0:T(1,128)S(1)} %get-tuple-element.244), channel_id=1, source_target_pairs={{1,0},{2,1},{3,2},{4,3},{5,4},{6,5},{7,6},{8,7},{9,8},{10,9},{11,1... | collective-permute-start | bytes 24584 | tf_op jit(solution)/shard_map/ppermute | solution.py:24
  179.0 8.3 %collective-permute-start.20 = (f32[4,1,512]{2,1,0:T(1,128)S(1)}, f32[4,1,512]{2,1,0:T(1,128)S(1)}, u32[]{:S(2)}, u32[]{:S(2)}) collective-permute-start(f32[4,1,512]{2,1,0:T(1,128)S(1)} %get-tuple-element.234), channel_id=1, source_target_pairs={{0,1},{1,2},{2,3},{3,4},{4,5},{5,6},{6,7},{7,8},{8,9},{9,10},{10,1... | collective-permute-start | bytes 24584 | tf_op jit(solution)/shard_map/ppermute | solution.py:22
  182.0 6.5 %collective-permute-start.21 = (f32[4,1,512]{2,1,0:T(1,128)S(1)}, f32[4,1,512]{2,1,0:T(1,128)S(1)}, u32[]{:S(2)}, u32[]{:S(2)}) collective-permute-start(f32[4,1,512]{2,1,0:T(1,128)S(1)} %get-tuple-element.235), channel_id=1, source_target_pairs={{1,0},{2,1},{3,2},{4,3},{5,4},{6,5},{7,6},{8,7},{9,8},{10,9},{11,1... | collective-permute-start | bytes 24584 | tf_op jit(solution)/shard_map/ppermute | solution.py:24
  189.4 8.3 %collective-permute-start.22 = (f32[4,1,512]{2,1,0:T(1,128)S(1)}, f32[4,1,512]{2,1,0:T(1,128)S(1)}, u32[]{:S(2)}, u32[]{:S(2)}) collective-permute-start(f32[4,1,512]{2,1,0:T(1,128)S(1)} %get-tuple-element.225), channel_id=1, source_target_pairs={{0,1},{1,2},{2,3},{3,4},{4,5},{5,6},{6,7},{7,8},{8,9},{9,10},{10,1... | collective-permute-start | bytes 24584 | tf_op jit(solution)/shard_map/ppermute | solution.py:22
  193.9 5.5 %collective-permute-start.23 = (f32[4,1,512]{2,1,0:T(1,128)S(1)}, f32[4,1,512]{2,1,0:T(1,128)S(1)}, u32[]{:S(2)}, u32[]{:S(2)}) collective-permute-start(f32[4,1,512]{2,1,0:T(1,128)S(1)} %get-tuple-element.226), channel_id=1, source_target_pairs={{1,0},{2,1},{3,2},{4,3},{5,4},{6,5},{7,6},{8,7},{9,8},{10,9},{11,1... | collective-permute-start | bytes 24584 | tf_op jit(solution)/shard_map/ppermute | solution.py:24
  200.4 8.1 %collective-permute-start.24 = (f32[4,1,512]{2,1,0:T(1,128)S(1)}, f32[4,1,512]{2,1,0:T(1,128)S(1)}, u32[]{:S(2)}, u32[]{:S(2)}) collective-permute-start(f32[4,1,512]{2,1,0:T(1,128)S(1)} %get-tuple-element.216), channel_id=1, source_target_pairs={{0,1},{1,2},{2,3},{3,4},{4,5},{5,6},{6,7},{7,8},{8,9},{9,10},{10,1... | collective-permute-start | bytes 24584 | tf_op jit(solution)/shard_map/ppermute | solution.py:22
  204.3 5.5 %collective-permute-start.25 = (f32[4,1,512]{2,1,0:T(1,128)S(1)}, f32[4,1,512]{2,1,0:T(1,128)S(1)}, u32[]{:S(2)}, u32[]{:S(2)}) collective-permute-start(f32[4,1,512]{2,1,0:T(1,128)S(1)} %get-tuple-element.217), channel_id=1, source_target_pairs={{1,0},{2,1},{3,2},{4,3},{5,4},{6,5},{7,6},{8,7},{9,8},{10,9},{11,1... | collective-permute-start | bytes 24584 | tf_op jit(solution)/shard_map/ppermute | solution.py:24
  210.7 8.3 %collective-permute-start.26 = (f32[4,1,512]{2,1,0:T(1,128)S(1)}, f32[4,1,512]{2,1,0:T(1,128)S(1)}, u32[]{:S(2)}, u32[]{:S(2)}) collective-permute-start(f32[4,1,512]{2,1,0:T(1,128)S(1)} %get-tuple-element.207), channel_id=1, source_target_pairs={{0,1},{1,2},{2,3},{3,4},{4,5},{5,6},{6,7},{7,8},{8,9},{9,10},{10,1... | collective-permute-start | bytes 24584 | tf_op jit(solution)/shard_map/ppermute | solution.py:22
  213.8 6.3 %collective-permute-start.27 = (f32[4,1,512]{2,1,0:T(1,128)S(1)}, f32[4,1,512]{2,1,0:T(1,128)S(1)}, u32[]{:S(2)}, u32[]{:S(2)}) collective-permute-start(f32[4,1,512]{2,1,0:T(1,128)S(1)} %get-tuple-element.208), channel_id=1, source_target_pairs={{1,0},{2,1},{3,2},{4,3},{5,4},{6,5},{7,6},{8,7},{9,8},{10,9},{11,1... | collective-permute-start | bytes 24584 | tf_op jit(solution)/shard_map/ppermute | solution.py:24
  221.0 8.3 %collective-permute-start.28 = (f32[4,1,512]{2,1,0:T(1,128)S(1)}, f32[4,1,512]{2,1,0:T(1,128)S(1)}, u32[]{:S(2)}, u32[]{:S(2)}) collective-permute-start(f32[4,1,512]{2,1,0:T(1,128)S(1)} %get-tuple-element.198), channel_id=1, source_target_pairs={{0,1},{1,2},{2,3},{3,4},{4,5},{5,6},{6,7},{7,8},{8,9},{9,10},{10,1... | collective-permute-start | bytes 24584 | tf_op jit(solution)/shard_map/ppermute | solution.py:22
  223.4 7.2 %collective-permute-start.29 = (f32[4,1,512]{2,1,0:T(1,128)S(1)}, f32[4,1,512]{2,1,0:T(1,128)S(1)}, u32[]{:S(2)}, u32[]{:S(2)}) collective-permute-start(f32[4,1,512]{2,1,0:T(1,128)S(1)} %get-tuple-element.199), channel_id=1, source_target_pairs={{1,0},{2,1},{3,2},{4,3},{5,4},{6,5},{7,6},{8,7},{9,8},{10,9},{11,1... | collective-permute-start | bytes 24584 | tf_op jit(solution)/shard_map/ppermute | solution.py:24
  231.5 8.3 %collective-permute-start.30 = (f32[4,1,512]{2,1,0:T(1,128)S(1)}, f32[4,1,512]{2,1,0:T(1,128)S(1)}, u32[]{:S(2)}, u32[]{:S(2)}) collective-permute-start(f32[4,1,512]{2,1,0:T(1,128)S(1)} %get-tuple-element.189), channel_id=1, source_target_pairs={{0,1},{1,2},{2,3},{3,4},{4,5},{5,6},{6,7},{7,8},{8,9},{9,10},{10,1... | collective-permute-start | bytes 24584 | tf_op jit(solution)/shard_map/ppermute | solution.py:22
  233.4 7.7 %collective-permute-start.31 = (f32[4,1,512]{2,1,0:T(1,128)S(1)}, f32[4,1,512]{2,1,0:T(1,128)S(1)}, u32[]{:S(2)}, u32[]{:S(2)}) collective-permute-start(f32[4,1,512]{2,1,0:T(1,128)S(1)} %get-tuple-element.190), channel_id=1, source_target_pairs={{1,0},{2,1},{3,2},{4,3},{5,4},{6,5},{7,6},{8,7},{9,8},{10,9},{11,1... | collective-permute-start | bytes 24584 | tf_op jit(solution)/shard_map/ppermute | solution.py:24
  241.9 8.3 %collective-permute-start.32 = (f32[4,1,512]{2,1,0:T(1,128)S(1)}, f32[4,1,512]{2,1,0:T(1,128)S(1)}, u32[]{:S(2)}, u32[]{:S(2)}) collective-permute-start(f32[4,1,512]{2,1,0:T(1,128)S(1)} %get-tuple-element.180), channel_id=1, source_target_pairs={{0,1},{1,2},{2,3},{3,4},{4,5},{5,6},{6,7},{7,8},{8,9},{9,10},{10,1... | collective-permute-start | bytes 24584 | tf_op jit(solution)/shard_map/ppermute | solution.py:22
  243.8 7.7 %collective-permute-start.33 = (f32[4,1,512]{2,1,0:T(1,128)S(1)}, f32[4,1,512]{2,1,0:T(1,128)S(1)}, u32[]{:S(2)}, u32[]{:S(2)}) collective-permute-start(f32[4,1,512]{2,1,0:T(1,128)S(1)} %get-tuple-element.181), channel_id=1, source_target_pairs={{1,0},{2,1},{3,2},{4,3},{5,4},{6,5},{7,6},{8,7},{9,8},{10,9},{11,1... | collective-permute-start | bytes 24584 | tf_op jit(solution)/shard_map/ppermute | solution.py:24
  252.4 8.3 %collective-permute-start.34 = (f32[4,1,512]{2,1,0:T(1,128)S(1)}, f32[4,1,512]{2,1,0:T(1,128)S(1)}, u32[]{:S(2)}, u32[]{:S(2)}) collective-permute-start(f32[4,1,512]{2,1,0:T(1,128)S(1)} %get-tuple-element.171), channel_id=1, source_target_pairs={{0,1},{1,2},{2,3},{3,4},{4,5},{5,6},{6,7},{7,8},{8,9},{9,10},{10,1... | collective-permute-start | bytes 24584 | tf_op jit(solution)/shard_map/ppermute | solution.py:22
  254.3 7.7 %collective-permute-start.35 = (f32[4,1,512]{2,1,0:T(1,128)S(1)}, f32[4,1,512]{2,1,0:T(1,128)S(1)}, u32[]{:S(2)}, u32[]{:S(2)}) collective-permute-start(f32[4,1,512]{2,1,0:T(1,128)S(1)} %get-tuple-element.172), channel_id=1, source_target_pairs={{1,0},{2,1},{3,2},{4,3},{5,4},{6,5},{7,6},{8,7},{9,8},{10,9},{11,1... | collective-permute-start | bytes 24584 | tf_op jit(solution)/shard_map/ppermute | solution.py:24
Sparse Core Ops, SparseCore 0:
  108.4 59.1 all-gather.1
where the time goes:
time: 273 us; the launch traced here: 272 us
  starting transfers between devices  149 us (55%)
  waiting for transfers between devices  41.5 us (15%)
  blocking collectives  35.7 us (13%)
  between operations  19.1 us (7%)
  other arithmetic  18.9 us (7%)
  local copies, waits for them, and re-layouts  7.54 us (3%)
    ppermute x18, starting transfers between devices, with_halo(): lax.ppermute(head, axis, [((i + 1) % count, i) for i in range(ends)])  99.1 us
    ppermute x18, starting transfers between devices, with_halo(): lax.ppermute(tail, axis, [(i, (i + 1) % count) for i in range(ends)])  49.7 us
    psum x1, blocking collectives, on_device(): score = lax.psum(local_score, 'domain') / (total_rows * width)  35.7 us
    ppermute x18, waiting for transfers between devices, with_halo(): lax.ppermute(head, axis, [((i + 1) % count, i) for i in range(ends)])  21.8 us
    all_gather x1, waiting for transfers between devices, on_device(): piece = lax.all_gather(before[None], 'member', axis=0, tiled=True)  19.7 us
    slice x36, local copies, waits for them, and re-layouts, gradients(): east = jnp.roll(middle, -1, axis=-1)  5.76 us
    add x18, other arithmetic, tendency(): advect = speed_u * grad_x + speed_v * grad_y  5.57 us
  transfers between devices with their start and end apart: 37, of which 18 were waited for; matrix products, arithmetic and copies ran while one was open for 2% of the time, Pallas kernels for 0%

commit v1 on v0

v1 whole, which is shorter than its diff:
```python
import jax
import jax.numpy as jnp
from jax import lax
from jax.experimental import pallas as pl
from jax.experimental.pallas import tpu as pltpu
from jax.sharding import PartitionSpec as P

F32 = jnp.float32
MESH = pl.DeviceIdType.MESH
STEPS = 3
STAGES = 3 * STEPS
time_step = 0.1
viscous = 0.05
coriolis = 1.0

FIELDS, CHUNKS, LANES = 4, 4, 128
OWN = 16
BUFFER_ROWS = 64
HALO = STAGES
PIECES = ((0, 16), (16, 16))


def stage(src, base, dst, start, groups, weight, old, lat0, lat1):
    lane = lax.broadcasted_iota(jnp.int32, (8, LANES), 1)
    row = lax.broadcasted_iota(jnp.int32, (8, LANES), 0).astype(F32)
    last, first = lane == LANES - 1, lane == 0
    keep = weight * (1.0 - 4.0 * viscous * time_step)
    spread = weight * viscous * time_step
    half = -weight * time_step * 0.5
    turn = weight * time_step * coriolis

    def body(group, carry):
        r = start + 8 * group
        here, north, south = pl.ds(r, 8), pl.ds(r + 1, 8), pl.ds(r - 1, 8)
        lat = ((row + r.astype(F32)) * lat1 + lat0) * turn
        cells = [[src[f, c, here, :] for c in range(CHUNKS)] for f in range(FIELDS)]
        to_west = [[pltpu.roll(cells[f][c], LANES - 1, 1) for c in range(CHUNKS)] for f in range(FIELDS)]
        to_east = [[pltpu.roll(cells[f][c], 1, 1) for c in range(CHUNKS)] for f in range(FIELDS)]
        for c in range(CHUNKS):
            E, W, N, S, dx, dy, out = [], [], [], [], [], [], []
            for f in range(FIELDS):
                e = jnp.where(last, to_west[f][(c + 1) % CHUNKS], to_west[f][c])
                w = jnp.where(first, to_east[f][(c - 1) % CHUNKS], to_east[f][c])
                n, s = src[f, c, north, :], src[f, c, south, :]
                E.append(e)
                W.append(w)
                N.append(n)
                S.append(s)
                dx.append(e - w)
                dy.append(n - s)
                o = keep * cells[f][c] + spread * ((e + w) + (n + s))
                if base is not None:
                    o = o + old * base[f, c, here, :]
                out.append(o)
            u, v = cells[1][c], cells[2][c]
            us, vs = half * u, half * v
            flux = (E[0] * E[1] - W[0] * W[1]) + (N[0] * N[2] - S[0] * S[2]) + (dx[1] + dy[2])
            dst[0, c, here, :] = out[0] + half * flux
            dst[1, c, here, :] = out[1] + (us * dx[1] + vs * dy[1]) + (lat * v + half * dx[0])
            dst[2, c, here, :] = out[2] + (us * dx[2] + vs * dy[2]) + (half * dy[0] - lat * u)
            dst[3, c, here, :] = out[3] + (us * dx[3] + vs * dy[3])
        return carry

    lax.fori_loop(0, groups, body, 0)


def kernel(
    parents, state, perturbation, after, score,
    A, C, S1, S2, noise, acc, got, *rest,
):
    pieces = len(PIECES)
    H, V, Q, X, T, U = (rest[i * pieces:(i + 1) * pieces] for i in range(6))
    (load_sem, halo_send, halo_recv, sum_send, sum_recv, out_sem,
     y_send, y_recv, x_send, x_recv, swap_send, swap_recv) = rest[6 * pieces:]
    m, d = lax.axis_index("member"), lax.axis_index("domain")
    y, xh, core = m // 4, (m // 2) % 2, m % 2
    xl, z = d // 8, d % 8
    rows = state.shape[2]
    domains = 16
    total_rows = rows * domains

    def member(y_, xh_, core_):
        return (y_ * 2 + xh_) * 2 + core_

    y_next, y_prev = (y + 1) % 4, (y + 3) % 4
    x_next = (member(y, (xh + xl) % 2, core), (1 - xl) * 8 + z)
    x_prev = (member(y, (xh + 1 - xl) % 2, core), (1 - xl) * 8 + z)
    other = (member(y, xh, 1 - core), d)
    d_next, d_prev = (m, (d + 1) % domains), (m, (d + domains - 1) % domains)

    def flip(size):
        return (m, d + size - 2 * size * ((d // size) % 2))

    sizes = (1, 2, 4, 8)
    greeted = [d_next, d_prev, x_next, x_prev, other] + [flip(s) for s in sizes]
    greeted += [(member(yy, xh, k), d) for yy in (y_next, y_prev) for k in (0, 1)]

    loads = []
    for c in range(CHUNKS):
        lanes = pl.ds(c * LANES, LANES)
        loads.append(pltpu.make_async_copy(state.at[0, :, :, lanes], A.at[:, c, pl.ds(OWN, rows), :], load_sem.at[0, c]))
    for c in range(CHUNKS):
        lanes = pl.ds(c * LANES, LANES)
        loads.append(pltpu.make_async_copy(perturbation.at[0, :, :, lanes], noise.at[:, c, :, :], load_sem.at[1, c]))
    for load in loads:
        load.start()

    barrier = pltpu.get_barrier_semaphore()
    for device in greeted:
        pl.semaphore_signal(barrier, inc=1, device_id=device, device_id_type=MESH)
    pl.semaphore_wait(barrier, len(greeted))

    def remote(src, dst, send, recv, device):
        copy = pltpu.make_async_remote_copy(
            src_ref=src, dst_ref=dst, send_sem=send, recv_sem=recv, device_id=device, device_id_type=MESH
        )
        copy.start()
        return copy

    def exchange(B, which):
        south = remote(B.at[:, :, pl.ds(OWN, HALO), :], B.at[:, :, pl.ds(OWN + rows, HALO), :],
                       halo_send.at[which, 0], halo_recv.at[which, 0], d_prev)
        north = remote(B.at[:, :, pl.ds(OWN + rows - HALO, HALO), :], B.at[:, :, pl.ds(OWN - HALO, HALO), :],
                       halo_send.at[which, 1], halo_recv.at[which, 1], d_next)
        south.wait()
        north.wait()

    nothing = jnp.zeros((FIELDS, CHUNKS, 8, LANES), F32)

    def clear_ends(B):
        @pl.when(d == 0)
        def _():
            B[:, :, pl.ds(OWN - 8, 8), :] = nothing

        @pl.when(d == domains - 1)
        def _():
            B[:, :, pl.ds(OWN + rows, 8), :] = nothing

    first_row = (d * rows - OWN).astype(F32)
    lat0 = 2.0 * (first_row + 0.5) / total_rows - 1.0
    lat1 = 2.0 / total_rows

    def run_steps(B):
        clear_ends(B)
        for k in range(1, STAGES + 1):
            groups = -(-(rows + 2 * (STAGES - k)) // 8)
            src, base, dst, weight, old = (
                (B, None, S1, 1.0, 0.0), (S1, B, S2, 0.25, 0.75), (S2, B, B, 2.0 / 3.0, 1.0 / 3.0)
            )[(k - 1) % 3]
            stage(src, base, dst, OWN - STAGES + k, groups, weight, old, lat0, lat1)
            if k < STAGES:
                clear_ends(dst)

    for load in loads:
        load.wait()
    exchange(A, 0)
    run_steps(A)

    pending = []
    mine, theirs = pl.ds(2 * core, 2), pl.ds(2 * (1 - core), 2)
    ring = []
    for i, (begin, count) in enumerate(PIECES):
        part = pl.ds(OWN + begin, count)
        place = H[i].at[y, core]
        local = pltpu.make_async_copy(A.at[mine, :, part, :], place, y_send.at[i, 7])
        local.start()
        copies = [local]
        for way, yy in enumerate((y_next, y_prev)):
            for k in (0, 1):
                copies.append(remote(A.at[pl.ds(2 * k, 2), :, part, :], place, y_send.at[i, 2 * way + k],
                                     y_recv.at[i, way, core], (member(yy, xh, k), d)))
        swap = remote(A.at[theirs, :, part, :], place, y_send.at[i, 4], y_recv.at[i, 2, 0], other)
        copies.append(swap)
        ring.append(copies)

    weight_row = lax.broadcasted_iota(jnp.int32, (8, LANES), 0).astype(F32)
    total = jnp.zeros((8, LANES), F32)
    for g in range(rows // 8):
        w = 1.0 + 2.0 * (weight_row + (d * rows + 8 * g).astype(F32)) / (total_rows - 1)
        q2 = jnp.zeros((8, LANES), F32)
        for c in range(CHUNKS):
            q = A[3, c, pl.ds(OWN + 8 * g, 8), :]
            q2 = q2 + q * q
        total = total + w * q2

    def add_up(step, total):
        acc[step] = total
        copy = remote(acc.at[step], got.at[step], sum_send.at[step], sum_recv.at[step], flip(sizes[step]))
        copy.wait()
        return total + got[step]

    for step in range(4):
        total = add_up(step, total)
    score[0] = jnp.sum(total) / (total_rows * state.shape[3])

    def arrived(buffer, sem):
        pltpu.make_async_copy(buffer, buffer, sem).wait()

    for i, (begin, count) in enumerate(PIECES):
        arrived(H[i].at[y_prev, 0], y_recv.at[i, 0, 0])
        on = remote(H[i].at[y_prev, 0], H[i].at[y_prev, 0], y_send.at[i, 5], y_recv.at[i, 2, 1], (member(y_next, xh, core), d))
        arrived(H[i].at[y_next, 1], y_recv.at[i, 1, 1])
        back = remote(H[i].at[y_next, 1], H[i].at[y_next, 1], y_send.at[i, 6], y_recv.at[i, 2, 2], (member(y_prev, xh, core), d))
        pending += [on, back]
    xs = []
    for i, (begin, count) in enumerate(PIECES):
        far = (y + 2) % 4
        arrived(H[i].at[y_prev, 1], y_recv.at[i, 0, 1])
        arrived(H[i].at[y_next, 0], y_recv.at[i, 1, 0])
        arrived(H[i].at[far, 0], y_recv.at[i, 2, 1])
        arrived(H[i].at[far, 1], y_recv.at[i, 2, 2])
        arrived(H[i].at[y, 1 - core], y_recv.at[i, 2, 0])
        ring[i][0].wait()
        for j in (0, 1):
            p = parents[member(y, 1 - xh, j)]
            V[i][j] = H[i][p // 4, p % 2]
            xs.append(remote(V[i].at[j], Q[i].at[j], x_send.at[i, j], x_recv.at[i, j], (x_next, x_prev)[j]))
    for i, (begin, count) in enumerate(PIECES):
        for j in (0, 1):
            arrived(Q[i].at[j], x_recv.at[i, j])
            pending.append(remote(Q[i].at[j], X[i].at[j], x_send.at[i, 2 + j], x_recv.at[i, 2 + j], (x_next, x_prev)[j]))
    swaps = []
    for i, (begin, count) in enumerate(PIECES):
        part = pl.ds(OWN + begin, count)
        for j in (0, 1):
            arrived(X[i].at[j], x_recv.at[i, 2 + j])
        p = parents[member(y, xh, 1 - core)]
        T[i][...] = jnp.where((p // 2) % 2 == xh, H[i][p // 4, p % 2], X[i][1 - core])
        swaps.append(remote(T[i], U[i], swap_send.at[i], swap_recv.at[i], other))
        p = parents[m]
        C[mine, :, part, :] = noise[mine, :, pl.ds(begin, count), :] + jnp.where(
            (p // 2) % 2 == xh, H[i][p // 4, p % 2], X[i][core])
    for i, (begin, count) in enumerate(PIECES):
        part = pl.ds(OWN + begin, count)
        swaps[i].wait()
        C[theirs, :, part, :] = noise[theirs, :, pl.ds(begin, count), :] + U[i][...]

    exchange(C, 1)
    run_steps(C)
    stores = []
    for c in range(CHUNKS):
        lanes = pl.ds(c * LANES, LANES)
        stores.append(pltpu.make_async_copy(C.at[:, c, pl.ds(OWN, rows), :], after.at[0, :, :, lanes], out_sem.at[c]))
    for store in stores:
        store.start()
    for copies in ring:
        for copy in copies[1:]:
            copy.wait_send()
    for copy in pending + xs:
        copy.wait_send()
    for store in stores:
        store.wait()


def solution(mesh):
    def on_device(state, perturbation, parents):
        rows = state.shape[2]
        buffer = pltpu.VMEM((FIELDS, CHUNKS, BUFFER_ROWS, LANES), F32)

        def each(*lead):
            return [pltpu.VMEM((*lead, 2, CHUNKS, count, LANES), F32) for _, count in PIECES]

        n = len(PIECES)
        dma = pltpu.SemaphoreType.DMA
        return pl.pallas_call(
            kernel,
            out_shape=(jax.ShapeDtypeStruct(state.shape, F32), jax.ShapeDtypeStruct((1,), F32)),
            in_specs=[
                pl.BlockSpec(memory_space=pltpu.SMEM),
                pl.BlockSpec(memory_space=pl.ANY),
                pl.BlockSpec(memory_space=pl.ANY),
            ],
            out_specs=(pl.BlockSpec(memory_space=pl.ANY), pl.BlockSpec(memory_space=pltpu.SMEM)),
            scratch_shapes=[buffer] * 4
            + [pltpu.VMEM((FIELDS, CHUNKS, rows, LANES), F32)]
            + [pltpu.VMEM((4, 8, LANES), F32)] * 2
            + each(4, 2) + each(2) + each(2) + each(2) + each() + each()
            + [dma((2, 4)), dma((2, 2)), dma((2, 2)), dma((4,)), dma((4,)), dma((4,)),
               dma((n, 8)), dma((n, 3, 3)), dma((n, 4)), dma((n, 4)), dma((n,)), dma((n,))],
            compiler_params=pltpu.CompilerParams(collective_id=0, has_side_effects=True),
        )(parents, state, perturbation)

    placed = P("member", None, "domain", None)
    return jax.shard_map(
        on_device, mesh=mesh, in_specs=(placed, placed, P()), out_specs=(placed, P("member")), check_vma=False
    )
```

time: 273 us -> 62.7 us (0.23)
  the two profiles are of different devices: /device:TPU:2 before, /device:TPU:1 now
where the time goes in v1:
time: 62.7 us; the launch traced here: 62.6 us
  Pallas kernels  58.5 us (93%)
  between operations  2.4 us (4%)
  local copies, waits for them, and re-layouts  1.67 us (3%)
    pallas_call x1, Pallas kernels, on_device(): pl.pallas_call(kernel, out_shape=(jax.ShapeDtypeStruct(state.shape, F32),...  58.5 us
    unnamed x1, local copies, waits for them, and re-layouts  1.67 us

profile of v1, /device:TPU:1, one launch (start us, length us, event | category | flops | bytes accessed | tf_op | source)
XLA Modules:
  0.0 62.6 jit_solution(8549205012972529947)
XLA Ops:
  0.6 58.5 %shard_map.50 = (f32[1,4,32,512]{3,2,1,0:T(8,128)}, f32[1]{0:T(128)}) custom-call(s32[16]{0:T(128)} %parents.1, f32[1,4,32,512]{3,2,1,0:T(8,128)} %state.1, f32[1,4,32,512]{3,2,1,0:T(8,128)} %perturbation.1), custom_call_target="tpu_custom_call" | custom-call | tf_op jit(solution)/shard_map/pallas_call | solution.py:265
  59.2 1.7 %copy.7 = f32[1,4,32,512]{3,2,1,0:T(8,128)} copy(f32[1,4,32,512]{3,2,1,0:T(8,128)} %get-tuple-element.4) | data formatting | bytes 524288

commit v2 on v1

v2 whole, which is shorter than its diff:
```python
import jax
import jax.numpy as jnp
from jax import lax
from jax.experimental import pallas as pl
from jax.experimental.pallas import tpu as pltpu
from jax.sharding import PartitionSpec as P

F32 = jnp.float32
MESH = pl.DeviceIdType.MESH
STEPS = 3
STAGES = 3 * STEPS
time_step = 0.1
viscous = 0.05
coriolis = 1.0

FIELDS, CHUNKS, LANES = 4, 4, 128
OWN = 16
BUFFER_ROWS = 64
HALO = STAGES
PIECES = ((0, 9), (23, 9), (9, 7), (16, 7))


def stage(src, base, dst, start, groups, weight, old, lat0, lat1):
    lane = lax.broadcasted_iota(jnp.int32, (8, LANES), 1)
    row = lax.broadcasted_iota(jnp.int32, (8, LANES), 0).astype(F32)
    last, first = lane == LANES - 1, lane == 0
    keep = weight * (1.0 - 4.0 * viscous * time_step)
    spread = weight * viscous * time_step
    half = -weight * time_step * 0.5
    turn = weight * time_step * coriolis

    def body(group, carry):
        r = start + 8 * group
        here, north, south = pl.ds(r, 8), pl.ds(r + 1, 8), pl.ds(r - 1, 8)
        lat = ((row + r.astype(F32)) * lat1 + lat0) * turn
        cells = [[src[f, c, here, :] for c in range(CHUNKS)] for f in range(FIELDS)]
        to_west = [[pltpu.roll(cells[f][c], LANES - 1, 1) for c in range(CHUNKS)] for f in range(FIELDS)]
        to_east = [[pltpu.roll(cells[f][c], 1, 1) for c in range(CHUNKS)] for f in range(FIELDS)]
        for c in range(CHUNKS):
            E, W, N, S, dx, dy, out = [], [], [], [], [], [], []
            for f in range(FIELDS):
                e = jnp.where(last, to_west[f][(c + 1) % CHUNKS], to_west[f][c])
                w = jnp.where(first, to_east[f][(c - 1) % CHUNKS], to_east[f][c])
                n, s = src[f, c, north, :], src[f, c, south, :]
                E.append(e)
                W.append(w)
                N.append(n)
                S.append(s)
                dx.append(e - w)
                dy.append(n - s)
                o = keep * cells[f][c] + spread * ((e + w) + (n + s))
                if base is not None:
                    o = o + old * base[f, c, here, :]
                out.append(o)
            u, v = cells[1][c], cells[2][c]
            us, vs = half * u, half * v
            flux = (E[0] * E[1] - W[0] * W[1]) + (N[0] * N[2] - S[0] * S[2]) + (dx[1] + dy[2])
            dst[0, c, here, :] = out[0] + half * flux
            dst[1, c, here, :] = out[1] + (us * dx[1] + vs * dy[1]) + (lat * v + half * dx[0])
            dst[2, c, here, :] = out[2] + (us * dx[2] + vs * dy[2]) + (half * dy[0] - lat * u)
            dst[3, c, here, :] = out[3] + (us * dx[3] + vs * dy[3])
        return carry

    lax.fori_loop(0, groups, body, 0)


def kernel(
    parents, state, perturbation, after, score,
    A, C, S1, S2, noise, acc, got, *rest,
):
    pieces = len(PIECES)
    H, V, X, T, U = (rest[i * pieces:(i + 1) * pieces] for i in range(5))
    (load_sem, halo_send, halo_recv, sum_send, sum_recv,
     y_send, y_recv, x_send, x_recv, swap_send, swap_recv) = rest[5 * pieces:]
    m, d = lax.axis_index("member"), lax.axis_index("domain")
    y, xh, core = m // 4, (m // 2) % 2, m % 2
    xl, z = d // 8, d % 8
    rows = state.shape[2]
    domains = 16
    total_rows = rows * domains

    def member(y_, xh_, core_):
        return (y_ * 2 + xh_) * 2 + core_

    y_next, y_prev = (y + 1) % 4, (y + 3) % 4
    across = (member(y, 1 - xh, core), d)
    other = (member(y, xh, 1 - core), d)
    d_next, d_prev = (m, (d + 1) % domains), (m, (d + domains - 1) % domains)

    def flip(size):
        return (m, d + size - 2 * size * ((d // size) % 2))

    sizes = (1, 2, 4, 8)
    greeted = [d_next, d_prev, across, other] + [flip(s) for s in sizes]
    greeted += [(member(yy, xh, k), d) for yy in (y_next, y_prev) for k in (0, 1)]

    loads = []
    for c in range(CHUNKS):
        lanes = pl.ds(c * LANES, LANES)
        loads.append(pltpu.make_async_copy(state.at[0, :, :, lanes], A.at[:, c, pl.ds(OWN, rows), :], load_sem.at[0, c]))
    for c in range(CHUNKS):
        lanes = pl.ds(c * LANES, LANES)
        loads.append(pltpu.make_async_copy(perturbation.at[0, :, :, lanes], noise.at[:, c, :, :], load_sem.at[1, c]))
    for load in loads:
        load.start()

    barrier = pltpu.get_barrier_semaphore()
    for device in greeted:
        pl.semaphore_signal(barrier, inc=1, device_id=device, device_id_type=MESH)
    pl.semaphore_wait(barrier, len(greeted))

    def remote(src, dst, send, recv, device):
        copy = pltpu.make_async_remote_copy(
            src_ref=src, dst_ref=dst, send_sem=send, recv_sem=recv, device_id=device, device_id_type=MESH
        )
        copy.start()
        return copy

    def send_south(B, which):
        return remote(B.at[:, :, pl.ds(OWN, HALO), :], B.at[:, :, pl.ds(OWN + rows, HALO), :],
                      halo_send.at[which, 0], halo_recv.at[which, 0], d_prev)

    def send_north(B, which):
        return remote(B.at[:, :, pl.ds(OWN + rows - HALO, HALO), :], B.at[:, :, pl.ds(OWN - HALO, HALO), :],
                      halo_send.at[which, 1], halo_recv.at[which, 1], d_next)

    nothing = jnp.zeros((FIELDS, CHUNKS, 8, LANES), F32)

    def clear_ends(B):
        @pl.when(d == 0)
        def _():
            B[:, :, pl.ds(OWN - 8, 8), :] = nothing

        @pl.when(d == domains - 1)
        def _():
            B[:, :, pl.ds(OWN + rows, 8), :] = nothing

    first_row = (d * rows - OWN).astype(F32)
    lat0 = 2.0 * (first_row + 0.5) / total_rows - 1.0
    lat1 = 2.0 / total_rows

    def run_steps(B, result):
        clear_ends(B)
        for k in range(1, STAGES + 1):
            groups = -(-(rows + 2 * (STAGES - k)) // 8)
            src, base, dst, weight, old = (
                (B, None, S1, 1.0, 0.0), (S1, B, S2, 0.25, 0.75), (S2, B, B, 2.0 / 3.0, 1.0 / 3.0)
            )[(k - 1) % 3]
            if k == STAGES:
                dst = result
            stage(src, base, dst, OWN - STAGES + k, groups, weight, old, lat0, lat1)
            if k < STAGES:
                clear_ends(dst)

    for load in loads:
        load.wait()
    halos = [send_south(A, 0), send_north(A, 0)]
    for halo in halos:
        halo.wait()
    run_steps(A, A)

    weight_row = lax.broadcasted_iota(jnp.int32, (8, LANES), 0).astype(F32)
    partial = [jnp.zeros((8, LANES), F32)]
    for g in range(rows // 8):
        w = 1.0 + 2.0 * (weight_row + (d * rows + 8 * g).astype(F32)) / (total_rows - 1)
        q2 = jnp.zeros((8, LANES), F32)
        for c in range(CHUNKS):
            q = A[3, c, pl.ds(OWN + 8 * g, 8), :]
            q2 = q2 + q * q
        partial[0] = partial[0] + w * q2
    sums = []

    def add_up():
        if sums:
            step = len(sums) - 1
            sums[-1].wait()
            partial[0] = partial[0] + got[step]
        step = len(sums)
        if step < len(sizes):
            acc[step] = partial[0]
            sums.append(remote(acc.at[step], got.at[step], sum_send.at[step], sum_recv.at[step], flip(sizes[step])))

    mine, theirs = pl.ds(2 * core, 2), pl.ds(2 * (1 - core), 2)
    far = (y + 2) % 4
    sent, local, swaps = [], [None] * pieces, [None] * pieces

    def arrived(buffer, sem):
        pltpu.make_async_copy(buffer, buffer, sem).wait()

    def ring(i):
        part = pl.ds(OWN + PIECES[i][0], PIECES[i][1])
        place = H[i].at[y, core]
        for way, yy in enumerate((y_next, y_prev)):
            for k in (0, 1):
                sent.append(remote(A.at[pl.ds(2 * k, 2), :, part, :], place, y_send.at[i, 2 * way + k],
                                   y_recv.at[i, way, core], (member(yy, xh, k), d)))
        sent.append(remote(A.at[theirs, :, part, :], place, y_send.at[i, 4], y_recv.at[i, 2, 0], other))
        local[i] = pltpu.make_async_copy(A.at[mine, :, part, :], place, y_send.at[i, 7])
        local[i].start()

    def forward(i):
        for way, (block, yy) in enumerate(((H[i].at[y_prev, 0], y_next), (H[i].at[y_next, 1], y_prev))):
            arrived(block, y_recv.at[i, way, way])
            sent.append(remote(block, block, y_send.at[i, 5 + way], y_recv.at[i, 2, 1 + way], (member(yy, xh, core), d)))

    def choose(i):
        arrived(H[i].at[y_prev, 1], y_recv.at[i, 0, 1])
        arrived(H[i].at[y_next, 0], y_recv.at[i, 1, 0])
        arrived(H[i].at[y, 1 - core], y_recv.at[i, 2, 0])
        local[i].wait()
        arrived(H[i].at[far, 0], y_recv.at[i, 2, 1])
        arrived(H[i].at[far, 1], y_recv.at[i, 2, 2])
        for j in (0, 1):
            p = parents[member(y, 1 - xh, j)]
            V[i][j] = H[i][p // 4, p % 2]
        sent.append(remote(V[i], X[i], x_send.at[i], x_recv.at[i], across))

    def swap(i):
        begin, count = PIECES[i]
        arrived(X[i], x_recv.at[i])
        p = parents[member(y, xh, 1 - core)]
        T[i][...] = jnp.where((p // 2) % 2 == xh, H[i][p // 4, p % 2], X[i][1 - core])
        swaps[i] = remote(T[i], U[i], swap_send.at[i], swap_recv.at[i], other)
        p = parents[m]
        C[mine, :, pl.ds(OWN + begin, count), :] = noise[mine, :, pl.ds(begin, count), :] + jnp.where(
            (p // 2) % 2 == xh, H[i][p // 4, p % 2], X[i][core])

    def finish(i):
        begin, count = PIECES[i]
        swaps[i].wait()
        C[theirs, :, pl.ds(OWN + begin, count), :] = noise[theirs, :, pl.ds(begin, count), :] + U[i][...]

    ring(0)
    ring(1)
    ring(2)
    add_up()
    forward(0)
    ring(3)
    forward(1)
    add_up()
    choose(0)
    forward(2)
    choose(1)
    swap(0)
    add_up()
    forward(3)
    finish(0)
    halos = [send_south(C, 1)]
    choose(2)
    swap(1)
    finish(1)
    halos.append(send_north(C, 1))
    add_up()
    choose(3)
    swap(2)
    finish(2)
    add_up()
    score[0] = jnp.sum(partial[0]) / (total_rows * state.shape[3])
    swap(3)
    finish(3)
    for halo in halos:
        halo.wait()

    class Result:
        def __setitem__(self, at, value):
            f, c, here, _ = at
            after[0, f, pl.ds(pl.multiple_of(here.start - OWN, 8), here.size), pl.ds(c * LANES, LANES)] = value

    run_steps(C, Result())
    for copy in sent:
        copy.wait_send()


def solution(mesh):
    def on_device(state, perturbation, parents):
        rows = state.shape[2]
        buffer = pltpu.VMEM((FIELDS, CHUNKS, BUFFER_ROWS, LANES), F32)

        def each(*lead):
            return [pltpu.VMEM((*lead, 2, CHUNKS, count, LANES), F32) for _, count in PIECES]

        n = len(PIECES)
        dma = pltpu.SemaphoreType.DMA
        return pl.pallas_call(
            kernel,
            out_shape=(pltpu.VMEM(state.shape, F32), jax.ShapeDtypeStruct((1,), F32)),
            in_specs=[
                pl.BlockSpec(memory_space=pltpu.SMEM),
                pl.BlockSpec(memory_space=pl.ANY),
                pl.BlockSpec(memory_space=pl.ANY),
            ],
            out_specs=(pl.BlockSpec(memory_space=pltpu.VMEM), pl.BlockSpec(memory_space=pltpu.SMEM)),
            scratch_shapes=[buffer] * 4
            + [pltpu.VMEM((FIELDS, CHUNKS, rows, LANES), F32)]
            + [pltpu.VMEM((4, 8, LANES), F32)] * 2
            + each(4, 2) + each(2) + each(2) + each() + each()
            + [dma((2, 4)), dma((2, 2)), dma((2, 2)), dma((4,)), dma((4,)),
               dma((n, 8)), dma((n, 3, 3)), dma((n,)), dma((n,)), dma((n,)), dma((n,))],
            compiler_params=pltpu.CompilerParams(collective_id=0, has_side_effects=True),
        )(parents, state, perturbation)

    placed = P("member", None, "domain", None)
    return jax.shard_map(
        on_device, mesh=mesh, in_specs=(placed, placed, P()), out_specs=(placed, P("member")), check_vma=False
    )
```

time: 62.7 us -> 52.7 us (0.84)
  Pallas kernels: 58.5 us -> 49.5 us
  local copies, waits for them, and re-layouts: 1.67 us -> 0.71 us
    pallas_call x1, Pallas kernels: 58.5 us -> 49.5 us  [on_device(): pl.pallas_call(kernel, out_shape=(pltpu.VMEM(state.shape, F32), jax.Shape...]
    unnamed x1, local copies, waits for them, and re-layouts: 1.67 us -> 0.71 us
where the time goes in v2:
time: 52.7 us; the launch traced here: 52.5 us
  Pallas kernels  49.5 us (94%)
  between operations  2.33 us (4%)
  local copies, waits for them, and re-layouts  0.71 us (1%)
    pallas_call x1, Pallas kernels, on_device(): pl.pallas_call(kernel, out_shape=(pltpu.VMEM(state.shape, F32), jax.Shape...  49.5 us

profile of v2, /device:TPU:1, one launch (start us, length us, event | category | flops | bytes accessed | tf_op | source)
XLA Modules:
  0.0 52.5 jit_solution(15838126631473697772)
XLA Ops:
  0.6 49.5 %shard_map.50 = (f32[1,4,32,512]{3,2,1,0:T(8,128)S(1)}, f32[1]{0:T(128)}) custom-call(s32[16]{0:T(128)} %parents.1, f32[1,4,32,512]{3,2,1,0:T(8,128)} %state.1, f32[1,4,32,512]{3,2,1,0:T(8,128)} %perturbation.1), custom_call_target="tpu_custom_call" | custom-call | tf_op jit(solution)/shard_map/pallas_call | solution.py:284
  50.2 0.7 %copy.7 = f32[1,4,32,512]{3,2,1,0:T(8,128)} copy(f32[1,4,32,512]{3,2,1,0:T(8,128)S(1)} %get-tuple-element.2) | data formatting | bytes 524288

commit v3 on v2

--- a/solution.py
+++ b/solution.py
@@ -17,10 +17,11 @@
 OWN = 16
 BUFFER_ROWS = 64
 HALO = STAGES
-PIECES = ((0, 9), (23, 9), (9, 7), (16, 7))
-
-
-def stage(src, base, dst, start, groups, weight, old, lat0, lat1):
+MIDDLE, TOP, BOTTOM = 0, 1, 2
+PIECES = ((9, 14), (0, 9), (23, 9))
+
+
+def stage(src, base, dst, start, rows, weight, old, lat0, lat1, shift=0):
     lane = lax.broadcasted_iota(jnp.int32, (8, LANES), 1)
     row = lax.broadcasted_iota(jnp.int32, (8, LANES), 0).astype(F32)
     last, first = lane == LANES - 1, lane == 0
@@ -30,8 +31,9 @@
     turn = weight * time_step * coriolis
 
     def body(group, carry):
-        r = start + 8 * group
+        r = jnp.minimum(start + 8 * group, start + rows - 8)
         here, north, south = pl.ds(r, 8), pl.ds(r + 1, 8), pl.ds(r - 1, 8)
+        there = pl.ds(r - shift, 8)
         lat = ((row + r.astype(F32)) * lat1 + lat0) * turn
         cells = [[src[f, c, here, :] for c in range(CHUNKS)] for f in range(FIELDS)]
         to_west = [[pltpu.roll(cells[f][c], LANES - 1, 1) for c in range(CHUNKS)] for f in range(FIELDS)]
@@ -55,18 +57,18 @@
             u, v = cells[1][c], cells[2][c]
             us, vs = half * u, half * v
             flux = (E[0] * E[1] - W[0] * W[1]) + (N[0] * N[2] - S[0] * S[2]) + (dx[1] + dy[2])
-            dst[0, c, here, :] = out[0] + half * flux
-            dst[1, c, here, :] = out[1] + (us * dx[1] + vs * dy[1]) + (lat * v + half * dx[0])
-            dst[2, c, here, :] = out[2] + (us * dx[2] + vs * dy[2]) + (half * dy[0] - lat * u)
-            dst[3, c, here, :] = out[3] + (us * dx[3] + vs * dy[3])
+            dst[0, c, there, :] = out[0] + half * flux
+            dst[1, c, there, :] = out[1] + (us * dx[1] + vs * dy[1]) + (lat * v + half * dx[0])
+            dst[2, c, there, :] = out[2] + (us * dx[2] + vs * dy[2]) + (half * dy[0] - lat * u)
+            dst[3, c, there, :] = out[3] + (us * dx[3] + vs * dy[3])
         return carry
 
-    lax.fori_loop(0, groups, body, 0)
+    lax.fori_loop(0, -(-rows // 8), body, 0)
 
 
 def kernel(
     parents, state, perturbation, after, score,
-    A, C, S1, S2, noise, acc, got, *rest,
+    A, C, Y, top, bottom, noise, acc, got, *rest,
 ):
     pieces = len(PIECES)
     H, V, X, T, U = (rest[i * pieces:(i + 1) * pieces] for i in range(5))
@@ -90,7 +92,7 @@
     def flip(size):
         return (m, d + size - 2 * size * ((d // size) % 2))
 
-    sizes = (1, 2, 4, 8)
+    sizes = (4, 8, 2, 1)
     greeted = [d_next, d_prev, across, other] + [flip(s) for s in sizes]
     greeted += [(member(yy, xh, k), d) for yy in (y_next, y_prev) for k in (0, 1)]
 
@@ -124,51 +126,63 @@
         return remote(B.at[:, :, pl.ds(OWN + rows - HALO, HALO), :], B.at[:, :, pl.ds(OWN - HALO, HALO), :],
                       halo_send.at[which, 1], halo_recv.at[which, 1], d_next)
 
+    first_row = (d * rows - OWN).astype(F32)
+    lat0 = 2.0 * (first_row + 0.5) / total_rows - 1.0
+    lat1 = 2.0 / total_rows
     nothing = jnp.zeros((FIELDS, CHUNKS, 8, LANES), F32)
 
-    def clear_ends(B):
+    def clear_south(B):
         @pl.when(d == 0)
         def _():
             B[:, :, pl.ds(OWN - 8, 8), :] = nothing
 
+    def clear_north(B):
         @pl.when(d == domains - 1)
         def _():
             B[:, :, pl.ds(OWN + rows, 8), :] = nothing
 
-    first_row = (d * rows - OWN).astype(F32)
-    lat0 = 2.0 * (first_row + 0.5) / total_rows - 1.0
-    lat1 = 2.0 / total_rows
-
-    def run_steps(B, result):
-        clear_ends(B)
-        for k in range(1, STAGES + 1):
-            groups = -(-(rows + 2 * (STAGES - k)) // 8)
-            src, base, dst, weight, old = (
-                (B, None, S1, 1.0, 0.0), (S1, B, S2, 0.25, 0.75), (S2, B, B, 2.0 / 3.0, 1.0 / 3.0)
-            )[(k - 1) % 3]
-            if k == STAGES:
-                dst = result
-            stage(src, base, dst, OWN - STAGES + k, groups, weight, old, lat0, lat1)
-            if k < STAGES:
-                clear_ends(dst)
-
-    for load in loads:
+    def run(B, first, count, k, dst=None, shift=0):
+        levels = [B] + [Y.at[i] for i in range(STAGES)]
+        weight, old = ((1.0, 0.0), (0.25, 0.75), (2.0 / 3.0, 1.0 / 3.0))[(k - 1) % 3]
+        base = levels[k - 1 - (k - 1) % 3] if old else None
+        stage(levels[k - 1], base, dst if dst is not None else levels[k], OWN + first, count, weight, old, lat0, lat1, shift)
+
+    def inside(B, until, stages):
+        for k in stages:
+            run(B, k, until - 2 * k, k)
+
+    def south(B, result, shift):
+        clear_south(B)
+        for k in range(1, STAGES):
+            run(B, k - STAGES, 16, k)
+            clear_south(Y.at[k - 1])
+        run(B, 0, 16, STAGES, result, shift)
+
+    def north(B, wide, result, shift):
+        clear_north(B)
+        for k in range(1, STAGES):
+            run(B, rows + STAGES - k - wide, wide, k)
+            clear_north(Y.at[k - 1])
+        run(B, rows - 16, 16, STAGES, result, shift)
+
+    for load in loads[:CHUNKS]:
         load.wait()
     halos = [send_south(A, 0), send_north(A, 0)]
-    for halo in halos:
-        halo.wait()
-    run_steps(A, A)
-
-    weight_row = lax.broadcasted_iota(jnp.int32, (8, LANES), 0).astype(F32)
-    partial = [jnp.zeros((8, LANES), F32)]
-    for g in range(rows // 8):
-        w = 1.0 + 2.0 * (weight_row + (d * rows + 8 * g).astype(F32)) / (total_rows - 1)
-        q2 = jnp.zeros((8, LANES), F32)
-        for c in range(CHUNKS):
-            q = A[3, c, pl.ds(OWN + 8 * g, 8), :]
-            q2 = q2 + q * q
-        partial[0] = partial[0] + w * q2
-    sums = []
+    inside(A, rows, range(1, STAGES + 1))
+
+    sums, partial = [], []
+
+    def weigh():
+        row = lax.broadcasted_iota(jnp.int32, (8, LANES), 0).astype(F32)
+        total = jnp.zeros((8, LANES), F32)
+        for g in range(rows // 8):
+            weight = 1.0 + 2.0 * (row + (d * rows + 8 * g).astype(F32)) / (total_rows - 1)
+            squares = jnp.zeros((8, LANES), F32)
+            for c in range(CHUNKS):
+                q = (top, bottom)[g // 2][3, c, pl.ds(8 * (g % 2), 8), :]
+                squares = squares + q * q
+            total = total + weight * squares
+        partial.append(total)
 
     def add_up():
         if sums:
@@ -188,7 +202,8 @@
         pltpu.make_async_copy(buffer, buffer, sem).wait()
 
     def ring(i):
-        part = pl.ds(OWN + PIECES[i][0], PIECES[i][1])
+        A, begin = ((Y.at[STAGES - 1], OWN + PIECES[i][0]), (top, 0), (bottom, 16 - PIECES[i][1]))[i]
+        part = pl.ds(begin, PIECES[i][1])
         place = H[i].at[y, core]
         for way, yy in enumerate((y_next, y_prev)):
             for k in (0, 1):
@@ -230,43 +245,47 @@
         swaps[i].wait()
         C[theirs, :, pl.ds(OWN + begin, count), :] = noise[theirs, :, pl.ds(begin, count), :] + U[i][...]
 
-    ring(0)
-    ring(1)
-    ring(2)
-    add_up()
-    forward(0)
-    ring(3)
-    forward(1)
-    add_up()
-    choose(0)
-    forward(2)
-    choose(1)
-    swap(0)
-    add_up()
-    forward(3)
-    finish(0)
+    ring(MIDDLE)
+    halos[1].wait()
+    south(A, top, OWN)
+    ring(TOP)
+    forward(MIDDLE)
+    halos[0].wait()
+    north(A, 16, bottom, OWN + 16)
+    ring(BOTTOM)
+    forward(TOP)
+    weigh()
+    add_up()
+    choose(MIDDLE)
+    choose(TOP)
+    forward(BOTTOM)
+    for load in loads[CHUNKS:]:
+        load.wait()
+    swap(MIDDLE)
+    swap(TOP)
+    choose(BOTTOM)
+    finish(MIDDLE)
+    finish(TOP)
     halos = [send_south(C, 1)]
-    choose(2)
-    swap(1)
-    finish(1)
+    add_up()
+    inside(C, PIECES[BOTTOM][0], range(1, STAGES))
+    swap(BOTTOM)
+    finish(BOTTOM)
     halos.append(send_north(C, 1))
     add_up()
-    choose(3)
-    swap(2)
-    finish(2)
-    add_up()
-    score[0] = jnp.sum(partial[0]) / (total_rows * state.shape[3])
-    swap(3)
-    finish(3)
-    for halo in halos:
-        halo.wait()
 
     class Result:
         def __setitem__(self, at, value):
             f, c, here, _ = at
-            after[0, f, pl.ds(pl.multiple_of(here.start - OWN, 8), here.size), pl.ds(c * LANES, LANES)] = value
-
-    run_steps(C, Result())
+            after[0, f, pl.ds(pl.multiple_of(here.start, 8), here.size), pl.ds(c * LANES, LANES)] = value
+
+    halos[0].wait()
+    north(C, 24, Result(), OWN)
+    add_up()
+    halos[1].wait()
+    south(C, Result(), OWN)
+    add_up()
+    score[0] = jnp.sum(partial[0]) / (total_rows * state.shape[3])
     for copy in sent:
         copy.wait_send()
 
@@ -290,7 +309,9 @@
                 pl.BlockSpec(memory_space=pl.ANY),
             ],
             out_specs=(pl.BlockSpec(memory_space=pltpu.VMEM), pl.BlockSpec(memory_space=pltpu.SMEM)),
-            scratch_shapes=[buffer] * 4
+            scratch_shapes=[buffer] * 2
+            + [pltpu.VMEM((STAGES, FIELDS, CHUNKS, BUFFER_ROWS, LANES), F32)]
+            + [pltpu.VMEM((FIELDS, CHUNKS, 16, LANES), F32)] * 2
             + [pltpu.VMEM((FIELDS, CHUNKS, rows, LANES), F32)]
             + [pltpu.VMEM((4, 8, LANES), F32)] * 2
             + each(4, 2) + each(2) + each(2) + each() + each()

time: 52.7 us -> 45.2 us (0.86)
  Pallas kernels: 49.5 us -> 42 us
    pallas_call x1, Pallas kernels: 49.5 us -> 42 us  [on_device(): pl.pallas_call(kernel, out_shape=(pltpu.VMEM(state.shape, F32), jax.Shape...]
where the time goes in v3:
time: 45.2 us; the launch traced here: 45.1 us
  Pallas kernels  42 us (93%)
  between operations  2.33 us (5%)
  local copies, waits for them, and re-layouts  0.71 us (2%)
    pallas_call x1, Pallas kernels, on_device(): pl.pallas_call(kernel, out_shape=(pltpu.VMEM(state.shape, F32), jax.Shape...  42 us

profile of v3, /device:TPU:1, one launch (start us, length us, event | category | flops | bytes accessed | tf_op | source)
XLA Modules:
  0.0 45.1 jit_solution(5249275258993034021)
XLA Ops:
  0.6 42.0 %shard_map.50 = (f32[1,4,32,512]{3,2,1,0:T(8,128)S(1)}, f32[1]{0:T(128)}) custom-call(s32[16]{0:T(128)} %parents.1, f32[1,4,32,512]{3,2,1,0:T(8,128)} %state.1, f32[1,4,32,512]{3,2,1,0:T(8,128)} %perturbation.1), custom_call_target="tpu_custom_call" | custom-call | tf_op jit(solution)/shard_map/pallas_call | solution.py:303
  42.7 0.7 %copy.7 = f32[1,4,32,512]{3,2,1,0:T(8,128)} copy(f32[1,4,32,512]{3,2,1,0:T(8,128)S(1)} %get-tuple-element.2) | data formatting | bytes 524288

commit v4 on v3

--- a/solution.py
+++ b/solution.py
@@ -71,9 +71,9 @@
     A, C, Y, top, bottom, noise, acc, got, *rest,
 ):
     pieces = len(PIECES)
-    H, V, X, T, U = (rest[i * pieces:(i + 1) * pieces] for i in range(5))
+    H, V, X = (rest[i * pieces:(i + 1) * pieces] for i in range(3))
     (load_sem, halo_send, halo_recv, sum_send, sum_recv,
-     y_send, y_recv, x_send, x_recv, swap_send, swap_recv) = rest[5 * pieces:]
+     y_send, y_recv, x_send, x_recv) = rest[3 * pieces:]
     m, d = lax.axis_index("member"), lax.axis_index("domain")
     y, xh, core = m // 4, (m // 2) % 2, m % 2
     xl, z = d // 8, d % 8
@@ -85,15 +85,13 @@
         return (y_ * 2 + xh_) * 2 + core_
 
     y_next, y_prev = (y + 1) % 4, (y + 3) % 4
-    across = (member(y, 1 - xh, core), d)
+    across = [(member(y, 1 - xh, k), d) for k in (0, 1)]
     other = (member(y, xh, 1 - core), d)
     d_next, d_prev = (m, (d + 1) % domains), (m, (d + domains - 1) % domains)
 
-    def flip(size):
-        return (m, d + size - 2 * size * ((d // size) % 2))
-
-    sizes = (4, 8, 2, 1)
-    greeted = [d_next, d_prev, across, other] + [flip(s) for s in sizes]
+    x_side, z_next, z_prev = (m, (1 - xl) * 8 + z), (m, xl * 8 + (z + 1) % 8), (m, xl * 8 + (z + 7) % 8)
+
+    greeted = [d_next, d_prev, z_next, z_prev, x_side, other] + across
     greeted += [(member(yy, xh, k), d) for yy in (y_next, y_prev) for k in (0, 1)]
 
     loads = []
@@ -158,11 +156,13 @@
             clear_south(Y.at[k - 1])
         run(B, 0, 16, STAGES, result, shift)
 
-    def north(B, wide, result, shift):
+    def north(B, wide, result, shift, meanwhile={}):
         clear_north(B)
         for k in range(1, STAGES):
             run(B, rows + STAGES - k - wide, wide, k)
             clear_north(Y.at[k - 1])
+            if k in meanwhile:
+                meanwhile[k]()
         run(B, rows - 16, 16, STAGES, result, shift)
 
     for load in loads[:CHUNKS]:
@@ -170,7 +170,7 @@
     halos = [send_south(A, 0), send_north(A, 0)]
     inside(A, rows, range(1, STAGES + 1))
 
-    sums, partial = [], []
+    sums = []
 
     def weigh():
         row = lax.broadcasted_iota(jnp.int32, (8, LANES), 0).astype(F32)
@@ -182,21 +182,25 @@
                 q = (top, bottom)[g // 2][3, c, pl.ds(8 * (g % 2), 8), :]
                 squares = squares + q * q
             total = total + weight * squares
-        partial.append(total)
+        acc[0] = total
 
     def add_up():
-        if sums:
-            step = len(sums) - 1
-            sums[-1].wait()
-            partial[0] = partial[0] + got[step]
         step = len(sums)
-        if step < len(sizes):
-            acc[step] = partial[0]
-            sums.append(remote(acc.at[step], got.at[step], sum_send.at[step], sum_recv.at[step], flip(sizes[step])))
+        for copy in sums[-1] if sums else ():
+            copy.wait()
+        if step == 0:
+            sums.append([remote(acc.at[0], acc.at[1], sum_send.at[0, 0], sum_recv.at[0, 0], x_side)])
+            return
+        if step == 1:
+            got[z] = acc[0] + acc[1]
+        if step <= 4:
+            ways = ((z_next, (z + 9 - step) % 8), (z_prev, (z + step - 1) % 8))
+            sums.append([remote(got.at[slot], got.at[slot], sum_send.at[step, way], sum_recv.at[step, way], device)
+                         for way, (device, slot) in enumerate(ways[:1] if step == 4 else ways)])
 
     mine, theirs = pl.ds(2 * core, 2), pl.ds(2 * (1 - core), 2)
     far = (y + 2) % 4
-    sent, local, swaps = [], [None] * pieces, [None] * pieces
+    sent, local = [], [None] * pieces
 
     def arrived(buffer, sem):
         pltpu.make_async_copy(buffer, buffer, sem).wait()
@@ -225,52 +229,45 @@
         local[i].wait()
         arrived(H[i].at[far, 0], y_recv.at[i, 2, 1])
         arrived(H[i].at[far, 1], y_recv.at[i, 2, 2])
-        for j in (0, 1):
-            p = parents[member(y, 1 - xh, j)]
+        for j, (home, device) in enumerate(((1 - xh, across[0]), (1 - xh, across[1]), (xh, other))):
+            p = parents[member(y, home, (0, 1, 1 - core)[j])]
             V[i][j] = H[i][p // 4, p % 2]
-        sent.append(remote(V[i], X[i], x_send.at[i], x_recv.at[i], across))
-
-    def swap(i):
+            slot = 2 if j == 2 else core
+            sent.append(remote(V[i].at[j], X[i].at[slot], x_send.at[i, j], x_recv.at[i, slot], device))
+
+    def take(i):
         begin, count = PIECES[i]
-        arrived(X[i], x_recv.at[i])
-        p = parents[member(y, xh, 1 - core)]
-        T[i][...] = jnp.where((p // 2) % 2 == xh, H[i][p // 4, p % 2], X[i][1 - core])
-        swaps[i] = remote(T[i], U[i], swap_send.at[i], swap_recv.at[i], other)
+        for slot in range(3):
+            arrived(X[i].at[slot], x_recv.at[i, slot])
         p = parents[m]
-        C[mine, :, pl.ds(OWN + begin, count), :] = noise[mine, :, pl.ds(begin, count), :] + jnp.where(
-            (p // 2) % 2 == xh, H[i][p // 4, p % 2], X[i][core])
-
-    def finish(i):
-        begin, count = PIECES[i]
-        swaps[i].wait()
-        C[theirs, :, pl.ds(OWN + begin, count), :] = noise[theirs, :, pl.ds(begin, count), :] + U[i][...]
+        near = (p // 2) % 2 == xh
+        into, add = pl.ds(OWN + begin, count), pl.ds(begin, count)
+        C[mine, :, into, :] = noise[mine, :, add, :] + jnp.where(near, H[i][p // 4, p % 2], X[i][core])
+        C[theirs, :, into, :] = noise[theirs, :, add, :] + jnp.where(near, X[i][2], X[i][1 - core])
 
     ring(MIDDLE)
     halos[1].wait()
     south(A, top, OWN)
     ring(TOP)
-    forward(MIDDLE)
     halos[0].wait()
-    north(A, 16, bottom, OWN + 16)
+    north(A, 16, bottom, OWN + 16, {5: lambda: forward(MIDDLE)})
     ring(BOTTOM)
     forward(TOP)
     weigh()
     add_up()
     choose(MIDDLE)
+    forward(BOTTOM)
     choose(TOP)
-    forward(BOTTOM)
+    add_up()
+    choose(BOTTOM)
     for load in loads[CHUNKS:]:
         load.wait()
-    swap(MIDDLE)
-    swap(TOP)
-    choose(BOTTOM)
-    finish(MIDDLE)
-    finish(TOP)
+    take(MIDDLE)
+    take(TOP)
     halos = [send_south(C, 1)]
     add_up()
     inside(C, PIECES[BOTTOM][0], range(1, STAGES))
-    swap(BOTTOM)
-    finish(BOTTOM)
+    take(BOTTOM)
     halos.append(send_north(C, 1))
     add_up()
 
@@ -285,7 +282,10 @@
     halos[1].wait()
     south(C, Result(), OWN)
     add_up()
-    score[0] = jnp.sum(partial[0]) / (total_rows * state.shape[3])
+    total = got[0]
+    for other_z in range(1, 8):
+        total = total + got[other_z]
+    score[0] = jnp.sum(total) / (total_rows * state.shape[3])
     for copy in sent:
         copy.wait_send()
 
@@ -313,10 +313,10 @@
             + [pltpu.VMEM((STAGES, FIELDS, CHUNKS, BUFFER_ROWS, LANES), F32)]
             + [pltpu.VMEM((FIELDS, CHUNKS, 16, LANES), F32)] * 2
             + [pltpu.VMEM((FIELDS, CHUNKS, rows, LANES), F32)]
-            + [pltpu.VMEM((4, 8, LANES), F32)] * 2
-            + each(4, 2) + each(2) + each(2) + each() + each()
-            + [dma((2, 4)), dma((2, 2)), dma((2, 2)), dma((4,)), dma((4,)),
-               dma((n, 8)), dma((n, 3, 3)), dma((n,)), dma((n,)), dma((n,)), dma((n,))],
+            + [pltpu.VMEM((2, 8, LANES), F32), pltpu.VMEM((8, 8, LANES), F32)]
+            + each(4, 2) + each(3) + each(3)
+            + [dma((2, 4)), dma((2, 2)), dma((2, 2)), dma((5, 2)), dma((5, 2)),
+               dma((n, 8)), dma((n, 3, 3)), dma((n, 3)), dma((n, 3))],
             compiler_params=pltpu.CompilerParams(collective_id=0, has_side_effects=True),
         )(parents, state, perturbation)
 

time: 45.2 us -> 43.5 us (0.962); the launches traced: 45.1 us -> 42.6 us
  Pallas kernels: 42 us -> 39.6 us
    pallas_call x1, Pallas kernels: 42 us -> 39.6 us  [on_device(): pl.pallas_call(kernel, out_shape=(pltpu.VMEM(state.shape, F32), jax.Shape...]
where the time goes in v4:
time: 43.5 us; the launch traced here: 42.6 us
  Pallas kernels  39.6 us (91%)
  between operations  2.33 us (5%)
  local copies, waits for them, and re-layouts  0.71 us (2%)
    pallas_call x1, Pallas kernels, on_device(): pl.pallas_call(kernel, out_shape=(pltpu.VMEM(state.shape, F32), jax.Shape...  39.6 us

profile of v4, /device:TPU:1, one launch (start us, length us, event | category | flops | bytes accessed | tf_op | source)
XLA Modules:
  0.0 42.6 jit_solution(5619915403135260495)
XLA Ops:
  0.6 39.6 %shard_map.50 = (f32[1,4,32,512]{3,2,1,0:T(8,128)S(1)}, f32[1]{0:T(128)}) custom-call(s32[16]{0:T(128)} %parents.1, f32[1,4,32,512]{3,2,1,0:T(8,128)} %state.1, f32[1,4,32,512]{3,2,1,0:T(8,128)} %perturbation.1), custom_call_target="tpu_custom_call" | custom-call | tf_op jit(solution)/shard_map/pallas_call | solution.py:303
  40.2 0.7 %copy.7 = f32[1,4,32,512]{3,2,1,0:T(8,128)} copy(f32[1,4,32,512]{3,2,1,0:T(8,128)S(1)} %get-tuple-element.2) | data formatting | bytes 524288

commit v5 on v4

--- a/solution.py
+++ b/solution.py
@@ -21,28 +21,43 @@
 PIECES = ((9, 14), (0, 9), (23, 9))
 
 
-def stage(src, base, dst, start, rows, weight, old, lat0, lat1, shift=0):
+def stage(src, base, dst, start, rows, weight, old, lat0, lat1, shift=0, edge=None):
     lane = lax.broadcasted_iota(jnp.int32, (8, LANES), 1)
-    row = lax.broadcasted_iota(jnp.int32, (8, LANES), 0).astype(F32)
+    whole_row = lax.broadcasted_iota(jnp.int32, (8, LANES), 0)
+    row = whole_row.astype(F32)
     last, first = lane == LANES - 1, lane == 0
     keep = weight * (1.0 - 4.0 * viscous * time_step)
     spread = weight * viscous * time_step
     half = -weight * time_step * 0.5
     turn = weight * time_step * coriolis
 
-    def body(group, carry):
-        r = jnp.minimum(start + 8 * group, start + rows - 8)
+    def one(r, low_high=None):
         here, north, south = pl.ds(r, 8), pl.ds(r + 1, 8), pl.ds(r - 1, 8)
         there = pl.ds(r - shift, 8)
+        if low_high is None:
+            clip = lambda out: out
+        else:
+            at = whole_row + r
+            valid = (at >= low_high[0]) & (at < low_high[1])
+            clip = lambda out: jnp.where(valid, out, 0.0)
         lat = ((row + r.astype(F32)) * lat1 + lat0) * turn
-        cells = [[src[f, c, here, :] for c in range(CHUNKS)] for f in range(FIELDS)]
-        to_west = [[pltpu.roll(cells[f][c], LANES - 1, 1) for c in range(CHUNKS)] for f in range(FIELDS)]
-        to_east = [[pltpu.roll(cells[f][c], 1, 1) for c in range(CHUNKS)] for f in range(FIELDS)]
+        cells, rolls = {}, {}
+
+        def cell(f, c):
+            if (f, c) not in cells:
+                cells[f, c] = src[f, c, here, :]
+            return cells[f, c]
+
+        def rolled(f, c, by):
+            if (f, c, by) not in rolls:
+                rolls[f, c, by] = pltpu.roll(cell(f, c), by, 1)
+            return rolls[f, c, by]
+
         for c in range(CHUNKS):
             E, W, N, S, dx, dy, out = [], [], [], [], [], [], []
             for f in range(FIELDS):
-                e = jnp.where(last, to_west[f][(c + 1) % CHUNKS], to_west[f][c])
-                w = jnp.where(first, to_east[f][(c - 1) % CHUNKS], to_east[f][c])
+                e = jnp.where(last, rolled(f, (c + 1) % CHUNKS, LANES - 1), rolled(f, c, LANES - 1))
+                w = jnp.where(first, rolled(f, (c - 1) % CHUNKS, 1), rolled(f, c, 1))
                 n, s = src[f, c, north, :], src[f, c, south, :]
                 E.append(e)
                 W.append(w)
@@ -50,25 +65,39 @@
                 S.append(s)
                 dx.append(e - w)
                 dy.append(n - s)
-                o = keep * cells[f][c] + spread * ((e + w) + (n + s))
+                o = keep * cell(f, c) + spread * ((e + w) + (n + s))
                 if base is not None:
                     o = o + old * base[f, c, here, :]
                 out.append(o)
-            u, v = cells[1][c], cells[2][c]
+            u, v = cell(1, c), cell(2, c)
             us, vs = half * u, half * v
             flux = (E[0] * E[1] - W[0] * W[1]) + (N[0] * N[2] - S[0] * S[2]) + (dx[1] + dy[2])
-            dst[0, c, there, :] = out[0] + half * flux
-            dst[1, c, there, :] = out[1] + (us * dx[1] + vs * dy[1]) + (lat * v + half * dx[0])
-            dst[2, c, there, :] = out[2] + (us * dx[2] + vs * dy[2]) + (half * dy[0] - lat * u)
-            dst[3, c, there, :] = out[3] + (us * dx[3] + vs * dy[3])
+            dst[0, c, there, :] = clip(out[0] + half * flux)
+            dst[1, c, there, :] = clip(out[1] + (us * dx[1] + vs * dy[1]) + (lat * v + half * dx[0]))
+            dst[2, c, there, :] = clip(out[2] + (us * dx[2] + vs * dy[2]) + (half * dy[0] - lat * u))
+            dst[3, c, there, :] = clip(out[3] + (us * dx[3] + vs * dy[3]))
+
+    groups = -(-rows // 8)
+
+    def two(pair, carry):
+        for group in (2 * pair, 2 * pair + 1):
+            one(jnp.minimum(start + 8 * group, start + rows - 8))
         return carry
 
-    lax.fori_loop(0, -(-rows // 8), body, 0)
+    if edge is not None:
+        for group in range(groups):
+            one(start + 8 * group, edge[1:] if group == edge[0] else None)
+        return
+
+    if groups > 1:
+        lax.fori_loop(0, groups // 2, two, 0)
+    if groups % 2:
+        one(start + rows - 8)
 
 
 def kernel(
-    parents, state, perturbation, after, score,
-    A, C, Y, top, bottom, noise, acc, got, *rest,
+    all_parents, state, perturbation, after, score,
+    parents, A, C, Y, top, bottom, noise, acc, got, *rest,
 ):
     pieces = len(PIECES)
     H, V, X = (rest[i * pieces:(i + 1) * pieces] for i in range(3))
@@ -90,9 +119,14 @@
     d_next, d_prev = (m, (d + 1) % domains), (m, (d + domains - 1) % domains)
 
     x_side, z_next, z_prev = (m, (1 - xl) * 8 + z), (m, xl * 8 + (z + 1) % 8), (m, xl * 8 + (z + 7) % 8)
+    z_next2, z_prev2 = (m, xl * 8 + (z + 2) % 8), (m, xl * 8 + (z + 6) % 8)
 
     greeted = [d_next, d_prev, z_next, z_prev, x_side, other] + across
     greeted += [(member(yy, xh, k), d) for yy in (y_next, y_prev) for k in (0, 1)]
+
+    barrier = pltpu.get_barrier_semaphore()
+    for device in greeted:
+        pl.semaphore_signal(barrier, inc=1, device_id=device, device_id_type=MESH)
 
     loads = []
     for c in range(CHUNKS):
@@ -101,12 +135,10 @@
     for c in range(CHUNKS):
         lanes = pl.ds(c * LANES, LANES)
         loads.append(pltpu.make_async_copy(perturbation.at[0, :, :, lanes], noise.at[:, c, :, :], load_sem.at[1, c]))
+    loads.append(pltpu.make_async_copy(all_parents, parents, load_sem.at[2, 0]))
     for load in loads:
         load.start()
 
-    barrier = pltpu.get_barrier_semaphore()
-    for device in greeted:
-        pl.semaphore_signal(barrier, inc=1, device_id=device, device_id_type=MESH)
     pl.semaphore_wait(barrier, len(greeted))
 
     def remote(src, dst, send, recv, device):
@@ -116,15 +148,24 @@
         copy.start()
         return copy
 
-    def send_south(B, which):
-        return remote(B.at[:, :, pl.ds(OWN, HALO), :], B.at[:, :, pl.ds(OWN + rows, HALO), :],
-                      halo_send.at[which, 0], halo_recv.at[which, 0], d_prev)
-
-    def send_north(B, which):
-        return remote(B.at[:, :, pl.ds(OWN + rows - HALO, HALO), :], B.at[:, :, pl.ds(OWN - HALO, HALO), :],
-                      halo_send.at[which, 1], halo_recv.at[which, 1], d_next)
+    def southward(B, which):
+        return pltpu.make_async_remote_copy(
+            src_ref=B.at[:, :, pl.ds(OWN, HALO), :], dst_ref=B.at[:, :, pl.ds(OWN + rows, HALO), :],
+            send_sem=halo_send.at[which, 0], recv_sem=halo_recv.at[which, 0], device_id=d_prev, device_id_type=MESH)
+
+    def northward(B, which):
+        return pltpu.make_async_remote_copy(
+            src_ref=B.at[:, :, pl.ds(OWN + rows - HALO, HALO), :], dst_ref=B.at[:, :, pl.ds(OWN - HALO, HALO), :],
+            send_sem=halo_send.at[which, 1], recv_sem=halo_recv.at[which, 1], device_id=d_next, device_id_type=MESH)
+
+    def at_south(act):
+        pl.when(d > 0)(act)
+
+    def at_north(act):
+        pl.when(d < domains - 1)(act)
 
     first_row = (d * rows - OWN).astype(F32)
+    nil = d // domains
     lat0 = 2.0 * (first_row + 0.5) / total_rows - 1.0
     lat1 = 2.0 / total_rows
     nothing = jnp.zeros((FIELDS, CHUNKS, 8, LANES), F32)
@@ -139,11 +180,14 @@
         def _():
             B[:, :, pl.ds(OWN + rows, 8), :] = nothing
 
-    def run(B, first, count, k, dst=None, shift=0):
+    low = jnp.where(d == 0, OWN, 0)
+    high = jnp.where(d == domains - 1, OWN + rows, BUFFER_ROWS)
+
+    def run(B, first, count, k, dst=None, shift=0, edge=None):
         levels = [B] + [Y.at[i] for i in range(STAGES)]
         weight, old = ((1.0, 0.0), (0.25, 0.75), (2.0 / 3.0, 1.0 / 3.0))[(k - 1) % 3]
         base = levels[k - 1 - (k - 1) % 3] if old else None
-        stage(levels[k - 1], base, dst if dst is not None else levels[k], OWN + first, count, weight, old, lat0, lat1, shift)
+        stage(levels[k - 1], base, dst if dst is not None else levels[k], OWN + first + nil, count, weight, old, lat0, lat1, shift, edge)
 
     def inside(B, until, stages):
         for k in stages:
@@ -152,22 +196,21 @@
     def south(B, result, shift):
         clear_south(B)
         for k in range(1, STAGES):
-            run(B, k - STAGES, 16, k)
-            clear_south(Y.at[k - 1])
+            run(B, k - STAGES, 16, k, edge=(0, low, BUFFER_ROWS))
         run(B, 0, 16, STAGES, result, shift)
 
     def north(B, wide, result, shift, meanwhile={}):
         clear_north(B)
         for k in range(1, STAGES):
-            run(B, rows + STAGES - k - wide, wide, k)
-            clear_north(Y.at[k - 1])
+            run(B, rows + STAGES - k - wide, wide, k, edge=(wide // 8 - 1, 0, high))
             if k in meanwhile:
                 meanwhile[k]()
         run(B, rows - 16, 16, STAGES, result, shift)
 
     for load in loads[:CHUNKS]:
         load.wait()
-    halos = [send_south(A, 0), send_north(A, 0)]
+    at_south(lambda: southward(A, 0).start())
+    at_north(lambda: northward(A, 0).start())
     inside(A, rows, range(1, STAGES + 1))
 
     sums = []
@@ -191,12 +234,17 @@
         if step == 0:
             sums.append([remote(acc.at[0], acc.at[1], sum_send.at[0, 0], sum_recv.at[0, 0], x_side)])
             return
+        plan = ()
         if step == 1:
             got[z] = acc[0] + acc[1]
-        if step <= 4:
-            ways = ((z_next, (z + 9 - step) % 8), (z_prev, (z + step - 1) % 8))
+            plan = ((z_next, z), (z_prev, z))
+        if step == 2:
+            plan = ((z_next2, z), (z_prev2, z), (z_next2, (z + 7) % 8), (z_prev2, (z + 1) % 8))
+        if step == 3:
+            plan = ((z_prev2, (z + 2) % 8),)
+        if plan:
             sums.append([remote(got.at[slot], got.at[slot], sum_send.at[step, way], sum_recv.at[step, way], device)
-                         for way, (device, slot) in enumerate(ways[:1] if step == 4 else ways)])
+                         for way, (device, slot) in enumerate(plan)])
 
     mine, theirs = pl.ds(2 * core, 2), pl.ds(2 * (1 - core), 2)
     far = (y + 2) % 4
@@ -246,29 +294,29 @@
         C[theirs, :, into, :] = noise[theirs, :, add, :] + jnp.where(near, X[i][2], X[i][1 - core])
 
     ring(MIDDLE)
-    halos[1].wait()
+    at_south(lambda: northward(A, 0).wait_recv())
     south(A, top, OWN)
     ring(TOP)
-    halos[0].wait()
+    at_north(lambda: southward(A, 0).wait_recv())
     north(A, 16, bottom, OWN + 16, {5: lambda: forward(MIDDLE)})
     ring(BOTTOM)
     forward(TOP)
     weigh()
     add_up()
+    for load in loads[CHUNKS:]:
+        load.wait()
     choose(MIDDLE)
     forward(BOTTOM)
     choose(TOP)
-    add_up()
     choose(BOTTOM)
-    for load in loads[CHUNKS:]:
-        load.wait()
+    add_up()
     take(MIDDLE)
     take(TOP)
-    halos = [send_south(C, 1)]
+    at_south(lambda: southward(C, 1).start())
     add_up()
     inside(C, PIECES[BOTTOM][0], range(1, STAGES))
     take(BOTTOM)
-    halos.append(send_north(C, 1))
+    at_north(lambda: northward(C, 1).start())
     add_up()
 
     class Result:
@@ -276,10 +324,9 @@
             f, c, here, _ = at
             after[0, f, pl.ds(pl.multiple_of(here.start, 8), here.size), pl.ds(c * LANES, LANES)] = value
 
-    halos[0].wait()
+    at_north(lambda: southward(C, 1).wait_recv())
     north(C, 24, Result(), OWN)
-    add_up()
-    halos[1].wait()
+    at_south(lambda: northward(C, 1).wait_recv())
     south(C, Result(), OWN)
     add_up()
     total = got[0]
@@ -288,6 +335,9 @@
     score[0] = jnp.sum(total) / (total_rows * state.shape[3])
     for copy in sent:
         copy.wait_send()
+    for which, B in enumerate((A, C)):
+        at_south(lambda: southward(B, which).wait_send())
+        at_north(lambda: northward(B, which).wait_send())
 
 
 def solution(mesh):
@@ -304,18 +354,19 @@
             kernel,
             out_shape=(pltpu.VMEM(state.shape, F32), jax.ShapeDtypeStruct((1,), F32)),
             in_specs=[
-                pl.BlockSpec(memory_space=pltpu.SMEM),
+                pl.BlockSpec(memory_space=pl.ANY),
                 pl.BlockSpec(memory_space=pl.ANY),
                 pl.BlockSpec(memory_space=pl.ANY),
             ],
             out_specs=(pl.BlockSpec(memory_space=pltpu.VMEM), pl.BlockSpec(memory_space=pltpu.SMEM)),
-            scratch_shapes=[buffer] * 2
+            scratch_shapes=[pltpu.SMEM(parents.shape, jnp.int32)]
+            + [buffer] * 2
             + [pltpu.VMEM((STAGES, FIELDS, CHUNKS, BUFFER_ROWS, LANES), F32)]
             + [pltpu.VMEM((FIELDS, CHUNKS, 16, LANES), F32)] * 2
             + [pltpu.VMEM((FIELDS, CHUNKS, rows, LANES), F32)]
             + [pltpu.VMEM((2, 8, LANES), F32), pltpu.VMEM((8, 8, LANES), F32)]
             + each(4, 2) + each(3) + each(3)
-            + [dma((2, 4)), dma((2, 2)), dma((2, 2)), dma((5, 2)), dma((5, 2)),
+            + [dma((3, 4)), dma((2, 2)), dma((2, 2)), dma((4, 4)), dma((4, 4)),
                dma((n, 8)), dma((n, 3, 3)), dma((n, 3)), dma((n, 3))],
             compiler_params=pltpu.CompilerParams(collective_id=0, has_side_effects=True),
         )(parents, state, perturbation)

time: 43.5 us -> 39.2 us (0.901)
  the two profiles are of different devices: /device:TPU:1 before, /device:TPU:2 now
where the time goes in v5:
time: 39.2 us; the launch traced here: 39.1 us
  Pallas kernels  36 us (92%)
  between operations  2.33 us (6%)
  local copies, waits for them, and re-layouts  0.71 us (2%)
    pallas_call x1, Pallas kernels, on_device(): pl.pallas_call(kernel, out_shape=(pltpu.VMEM(state.shape, F32), jax.Shape...  36 us

profile of v5, /device:TPU:2, one launch (start us, length us, event | category | flops | bytes accessed | tf_op | source)
XLA Modules:
  0.0 39.1 jit_solution(14047258745194781921)
XLA Ops:
  0.6 36.0 %shard_map.50 = (f32[1,4,32,512]{3,2,1,0:T(8,128)S(1)}, f32[1]{0:T(128)}) custom-call(s32[16]{0:T(128)} %all_parents.1, f32[1,4,32,512]{3,2,1,0:T(8,128)} %state.1, f32[1,4,32,512]{3,2,1,0:T(8,128)} %perturbation.1), custom_call_target="tpu_custom_call" | custom-call | tf_op jit(solution)/shard_map/pallas_call | solution.py:353
  36.7 0.7 %copy.7 = f32[1,4,32,512]{3,2,1,0:T(8,128)} copy(f32[1,4,32,512]{3,2,1,0:T(8,128)S(1)} %get-tuple-element.2) | data formatting | bytes 524288
